TPU v7x, 128 devices: a whole 4x4x4 slice. The times are simulated.
128 devices in a mesh: section: 8 (over y, core), hid: 16 (over z, x).
Axes of the slice: x: 4, y: 4, z: 4, core: 2. Of those that a mesh axis runs over, the one named last changes fastest.
Arguments:
- streams: float32 [8, 2, 512, 1024], P('section', None, 'hid'), may hold values from -6 to 6
- cotangents: float32 [8, 2, 512, 1024], P('section', None, 'hid'), may hold values from -0.6 to 0.6
- feed_streams: float32 [2, 2, 512, 1024], P(None, None, 'hid'), may hold values from -6 to 6
- feed_cotangents: float32 [2, 2, 512, 1024], P(None, None, 'hid'), may hold values from -0.6 to 0.6
- w_in: bfloat16 [8, 1024, 16384], P('section', None, 'hid'), may hold values from -0.1875 to 0.1875
- w_out: bfloat16 [8, 16384, 1024], P('section', 'hid'), may hold values from -0.046875 to 0.046875
- gain: float32 [8, 1024], P('section'), may hold values from 0.1 to 1.9
Outputs:
- out_streams: float32 [8, 2, 512, 1024], P('section', None, 'hid')
- out_cotangents: float32 [8, 2, 512, 1024], P('section', None, 'hid')
- grad_in: float32 [8, 1024, 16384], P('section', None, 'hid')
- grad_out: float32 [8, 16384, 1024], P('section', 'hid')
All inputs are finite; a program needn't handle non-finite values.
Results may differ from a plain program's by a relative error of at most 0.0071.
Values may be sent and summed in bfloat16 or wider, within the bound.
A program may use at most 128 MiB of HBM per device.

v0:
```python
from functools import partial

import jax
import jax.numpy as jnp
from jax import lax
from jax.sharding import PartitionSpec as P


def from_behind(value, axis, steps):
    count = lax.axis_size(axis)
    initial, last = (max(0, -steps), min(count, count - steps))
    return lax.ppermute(value, axis, [(source, source + steps) for source in range(initial, last)])


def sent_to_all(array, axis):
    copies = jnp.broadcast_to(array, (lax.axis_size(axis), *array.shape))
    return lax.all_to_all(copies, axis, split_axis=0, concat_axis=0, tiled=True)


def in_order(blocks, dim):
    blocks = jnp.moveaxis(blocks, 0, dim)
    dims = blocks.shape
    return blocks.reshape(*dims[:dim], dims[dim] * dims[dim + 1], *dims[dim + 2 :])


def gather_directly(array, axis, dim):
    blocks = sent_to_all(array, axis)
    return in_order(blocks, dim)


def in_one_piece(arrays, axis, dim, along):
    widths = [a.shape[along] for a in arrays]
    both = jnp.concatenate(arrays, axis=along)
    out = gather_directly(both, axis, dim)
    return tuple(jnp.split(out, [sum(widths[:k]) for k in range(1, len(widths))], axis=along))


def in_blocks(array, dim, devices):
    dims = array.shape
    blocks = array.reshape(*dims[:dim], devices, dims[dim] // devices, *dims[dim + 1 :])
    return jnp.moveaxis(blocks, dim, 0)


def sent_and_summed(array, axis, dim):
    devices = lax.axis_size(axis)
    blocks = lax.all_to_all(in_blocks(array, dim, devices), axis, 0, 0, tiled=True)
    return jnp.sum(blocks, axis=0)


def normalize(stream):
    mean_sq = jnp.mean(stream * stream, axis=-1, keepdims=True)
    scale_row = lax.rsqrt(mean_sq + 1e-06)
    return (stream * scale_row, scale_row)


def shards(streams, cotangents, feed_streams, feed_cotangents, w_in, w_out, gain):
    held = streams[0]
    held_cot = cotangents[0]
    weight_in = w_in[0]
    weight_out = w_out[0]
    gain_row = gain[0]
    section_idx = lax.axis_index("section")
    top_section = lax.axis_size("section") - 1
    width = held.shape[2]
    total_in = jnp.zeros(weight_in.shape, jnp.float32)
    total_out = jnp.zeros(weight_out.shape, jnp.float32)
    tick_count = feed_streams.shape[0] + 1
    for tick_num in range(tick_count):
        first, second = (held[0], held[1])
        grad_first, grad_second = (held_cot[0], held_cot[1])
        normed, scale_row = normalize(first)
        lifted = (normed * gain_row).astype(jnp.bfloat16)
        cotan = grad_second.astype(jnp.bfloat16)
        if tick_num < tick_count - 1:
            passed = from_behind(jnp.stack([first, grad_second]), "section", -1)
        full_lift, full_cot = in_one_piece((lifted, cotan), "hid", 0, 1)
        pre = jnp.dot(full_lift, weight_in, preferred_element_type=jnp.float32)
        hidden = jax.nn.gelu(pre, approximate=True).astype(jnp.bfloat16)
        back_hidden = jnp.dot(full_cot, weight_out.T, preferred_element_type=jnp.float32)
        unused, pull = jax.vjp(partial(jax.nn.gelu, approximate=True), pre)
        back_pre = pull(back_hidden)[0].astype(jnp.bfloat16)
        summed = sent_and_summed(
            jnp.concatenate(
                [
                    jnp.dot(hidden, weight_out, preferred_element_type=jnp.float32),
                    jnp.dot(back_pre, weight_in.T, preferred_element_type=jnp.float32),
                ],
                axis=1,
            ),
            "hid",
            0,
        )
        block_out = summed[:, :width]
        back_lift = summed[:, width:]
        restored = second - block_out
        back_norm = back_lift * gain_row
        grad_stream = grad_first + scale_row * (
            back_norm - normed * jnp.mean(back_norm * normed, axis=-1, keepdims=True)
        )
        total_in = total_in + jnp.dot(full_lift.T, back_pre, preferred_element_type=jnp.float32)
        total_out = total_out + jnp.dot(hidden.T, full_cot, preferred_element_type=jnp.float32)
        new_streams = jnp.stack([restored, first])
        new_cot = jnp.stack([grad_second, grad_stream])
        if tick_num < tick_count - 1:
            changed = from_behind(jnp.stack([restored, grad_stream]), "section", -1)
            moved_streams = jnp.stack([changed[0], passed[0]])
            moved_cot = jnp.stack([passed[1], changed[1]])
            at_top = section_idx == top_section
            held = jnp.where(at_top, feed_streams[tick_num], moved_streams)
            held_cot = jnp.where(at_top, feed_cotangents[tick_num], moved_cot)
    return (new_streams[None], new_cot[None], total_in[None], total_out[None])


def solution(mesh):
    placed = (
        P("section", None, "hid", None),
        P("section", None, "hid", None),
        P(None, None, "hid", None),
        P(None, None, "hid", None),
        P("section", None, "hid"),
        P("section", "hid", None),
        P("section", None),
    )
    return jax.shard_map(
        shards,
        mesh=mesh,
        in_specs=placed,
        out_specs=(
            P("section", None, "hid", None),
            P("section", None, "hid", None),
            P("section", None, "hid"),
            P("section", "hid", None),
        ),
        check_vma=False,
    )
```

profile of v0, /device:TPU:8, one launch (start us, length us, event | category | flops | bytes accessed | tf_op | source)
XLA Modules:
  0.0 364.8 jit_solution(11638104324825108224)
XLA Ops:
  4.0 36.2 %all_to_all.30 = bf16[16,32,2048]{2,1,0:T(8,128)(2,1)S(1)} all-to-all(bf16[16,32,2048]{2,1,0:T(8,128)(2,1)S(1)} %broadcast_in_dim.27), channel_id=1, replica_groups=mesh['section'=8,'hid'=16] {'hid'}, dimensions={0} | all-to-all | bytes 4194304 | tf_op jit(solution)/shard_map/all_to_all | solution.py:17
  41.5 2.4 fusion.6
  44.0 1.4 fusion.31
  46.7 2.5 pad_maximum_fusion
  49.2 4.7 %all-to-all-start.1 = ((f32[16,32,2048]{2,1,0:T(8,128)}), f32[16,32,2048]{2,1,0:T(8,128)}, u32[]{:S(2)}, u32[]{:S(2)}) async-start(f32[16,32,2048]{2,1,0:T(8,128)} %bitcast.143), calls=%async_computation.1 | async-start | bytes 8388608 | tf_op jit(solution)/shard_map/all_to_all | solution.py:46
  54.7 2.0 collective-permute-start.1
  56.7 57.5 %all-to-all-done.1 = f32[16,32,2048]{2,1,0:T(8,128)} async-done(((f32[16,32,2048]{2,1,0:T(8,128)}), f32[16,32,2048]{2,1,0:T(8,128)}, u32[]{:S(2)}, u32[]{:S(2)}) %all-to-all-start.1) | async-done | bytes 4194336 | tf_op jit(solution)/shard_map/all_to_all | solution.py:46
  114.2 2.4 reduce_sum.82
  118.6 1.9 collective-permute-start
  121.5 3.2 collective-permute-done
  126.3 33.5 %all_to_all.31 = bf16[16,32,2048]{2,1,0:T(8,128)(2,1)S(1)} all-to-all(bf16[16,32,2048]{2,1,0:T(8,128)(2,1)S(1)} %broadcast_in_dim.28), channel_id=1, replica_groups=mesh['section'=8,'hid'=16] {'hid'}, dimensions={0} | all-to-all | bytes 4194304 | tf_op jit(solution)/shard_map/all_to_all | solution.py:17
  161.1 2.4 fusion.13
  163.5 1.4 fusion.27
  166.2 2.5 pad_maximum_fusion.1
  168.7 4.5 %all-to-all-start.3 = ((f32[16,32,2048]{2,1,0:T(8,128)}), f32[16,32,2048]{2,1,0:T(8,128)}, u32[]{:S(2)}, u32[]{:S(2)}) async-start(f32[16,32,2048]{2,1,0:T(8,128)} %bitcast.144), calls=%async_computation.3 | async-start | bytes 8388608 | tf_op jit(solution)/shard_map/all_to_all | solution.py:46
  174.0 1.9 collective-permute-start.3
  176.0 61.8 %all-to-all-done.3 = f32[16,32,2048]{2,1,0:T(8,128)} async-done(((f32[16,32,2048]{2,1,0:T(8,128)}), f32[16,32,2048]{2,1,0:T(8,128)}, u32[]{:S(2)}, u32[]{:S(2)}) %all-to-all-start.3) | async-done | bytes 4194336 | tf_op jit(solution)/shard_map/all_to_all | solution.py:46
  237.7 2.4 reduce_sum.85
  240.5 1.9 collective-permute-start.2
  243.4 2.9 collective-permute-done.2
  246.9 33.3 %all_to_all.32 = bf16[16,32,2048]{2,1,0:T(8,128)(2,1)S(1)} all-to-all(bf16[16,32,2048]{2,1,0:T(8,128)(2,1)S(1)} %broadcast_in_dim.29), channel_id=1, replica_groups=mesh['section'=8,'hid'=16] {'hid'}, dimensions={0} | all-to-all | bytes 4194304 | tf_op jit(solution)/shard_map/all_to_all | solution.py:17
  281.6 2.4 fusion.20
  284.0 1.4 fusion.23
  286.8 2.5 pad_maximum_fusion.2
  289.2 4.8 %all-to-all-start.5 = ((f32[16,32,2048]{2,1,0:T(8,128)}), f32[16,32,2048]{2,1,0:T(8,128)}, u32[]{:S(2)}, u32[]{:S(2)}) async-start(f32[16,32,2048]{2,1,0:T(8,128)} %bitcast.142), calls=%async_computation.5 | async-start | bytes 8388608 | tf_op jit(solution)/shard_map/all_to_all | solution.py:46
  294.1 3.0 fusion.64
  297.1 1.5 fusion.61
  300.5 1.5 fusion.55
  302.4 3.4 add_bitcast_fusion.1
  305.7 3.6 add_bitcast_fusion
  309.4 51.3 %all-to-all-done.5 = f32[16,32,2048]{2,1,0:T(8,128)} async-done(((f32[16,32,2048]{2,1,0:T(8,128)}), f32[16,32,2048]{2,1,0:T(8,128)}, u32[]{:S(2)}, u32[]{:S(2)}) %all-to-all-start.5) | async-done | bytes 4194336 | tf_op jit(solution)/shard_map/all_to_all | solution.py:46
  360.6 2.4 reduce_sum.88
  (107 shorter events, 23.1 us)
Async XLA Ops:
  0.6 40.9 %copy-start = (bf16[1,1024,1024]{2,1,0:T(8,128)(2,1)S(1)}, bf16[1,1024,1024]{2,1,0:T(8,128)(2,1)}, u32[]{:S(2)}) copy-start(bf16[1,1024,1024]{2,1,0:T(8,128)(2,1)} %param.12) | copy-start | bytes 6291460
  4.0 36.2 %copy-start.19 = (bf16[1,1024,1024]{2,1,0:T(8,128)(2,1)S(1)}, bf16[1,1024,1024]{2,1,0:T(8,128)(2,1)}, u32[]{:S(2)}) copy-start(bf16[1,1024,1024]{2,1,0:T(8,128)(2,1)} %param.11) | copy-start | bytes 6291460
  41.5 2.4 copy-start.22
  43.9 1.5 copy-start.12
  49.2 4.7 %copy-start.17 = (f32[1,2,32,1024]{3,2,1,0:T(8,128)S(1)}, f32[1,2,32,1024]{3,2,1,0:T(8,128)}, u32[]{:S(2)}) copy-start(f32[1,2,32,1024]{3,2,1,0:T(8,128)} %param.8) | copy-start | bytes 786436
  49.2 4.7 %copy-start.7 = (f32[1,2,32,1024]{3,2,1,0:T(8,128)S(1)}, f32[1,2,32,1024]{3,2,1,0:T(8,128)}, u32[]{:S(2)}) copy-start(f32[1,2,32,1024]{3,2,1,0:T(8,128)} %param.7) | copy-start | bytes 786436
  49.2 65.0 %all-to-all-start.1 = ((f32[16,32,2048]{2,1,0:T(8,128)}), f32[16,32,2048]{2,1,0:T(8,128)}, u32[]{:S(2)}, u32[]{:S(2)}) async-start(f32[16,32,2048]{2,1,0:T(8,128)} %bitcast.143), calls=%async_computation.1 | async-start | bytes 8388608 | tf_op jit(solution)/shard_map/all_to_all | solution.py:46
  54.7 62.0 %copy-start.18 = (f32[1,1024]{1,0:T(1,128)S(1)}, f32[1,1024]{1,0:T(1,128)}, u32[]{:S(2)}) copy-start(f32[1,1024]{1,0:T(1,128)} %param.13) | copy-start | bytes 12292
  54.7 65.8 %collective-permute-start.1 = (f32[2,32,1024]{2,1,0:T(8,128)}, f32[2,32,1024]{2,1,0:T(8,128)}, u32[]{:S(2)}, u32[]{:S(2)}) collective-permute-start(f32[2,32,1024]{2,1,0:T(8,128)} %pad_maximum_fusion.4), channel_id=1, source_target_pairs={{16,0},{32,16},{48,32},{64,48},{80,64},{96,80},{112,96},{17,1},{33... | collective-permute-start | bytes 786440 | tf_op jit(solution)/shard_map/ppermute | solution.py:12
  116.6 8.1 %copy-start.15 = (f32[2,2,32,1024]{3,2,1,0:T(8,128)S(1)}, f32[2,2,32,1024]{3,2,1,0:T(8,128)}, u32[]{:S(2)}) copy-start(f32[2,2,32,1024]{3,2,1,0:T(8,128)} %param.9) | copy-start | bytes 1572868
  118.6 6.1 %collective-permute-start = (f32[2,32,1024]{2,1,0:T(8,128)}, f32[2,32,1024]{2,1,0:T(8,128)S(1)}, u32[]{:S(2)}, u32[]{:S(2)}) collective-permute-start(f32[2,32,1024]{2,1,0:T(8,128)} %pad_maximum_fusion.3), channel_id=1, source_target_pairs={{16,0},{32,16},{48,32},{64,48},{80,64},{96,80},{112,96},{17,1},{33... | collective-permute-start | bytes 786440 | tf_op jit(solution)/shard_map/ppermute | solution.py:12
  126.2 33.5 %copy-start.20 = (bf16[1,1024,1024]{2,1,0:T(8,128)(2,1)S(1)}, bf16[1,1024,1024]{2,1,0:T(8,128)(2,1)}, u32[]{:S(2)}) copy-start(bf16[1,1024,1024]{2,1,0:T(8,128)(2,1)} %param.11) | copy-start | bytes 6291460
  159.7 1.3 copy-start.5
  161.1 2.4 copy-start.24
  163.5 1.5 copy-start.13
  168.7 69.0 %all-to-all-start.3 = ((f32[16,32,2048]{2,1,0:T(8,128)}), f32[16,32,2048]{2,1,0:T(8,128)}, u32[]{:S(2)}, u32[]{:S(2)}) async-start(f32[16,32,2048]{2,1,0:T(8,128)} %bitcast.144), calls=%async_computation.3 | async-start | bytes 8388608 | tf_op jit(solution)/shard_map/all_to_all | solution.py:46
  174.0 68.4 %collective-permute-start.3 = (f32[2,32,1024]{2,1,0:T(8,128)}, f32[2,32,1024]{2,1,0:T(8,128)}, u32[]{:S(2)}, u32[]{:S(2)}) collective-permute-start(f32[2,32,1024]{2,1,0:T(8,128)} %pad_maximum_fusion.6), channel_id=1, source_target_pairs={{16,0},{32,16},{48,32},{64,48},{80,64},{96,80},{112,96},{17,1},{33... | collective-permute-start | bytes 786440 | tf_op jit(solution)/shard_map/ppermute | solution.py:12
  240.1 6.4 %copy-start.16 = (f32[2,2,32,1024]{3,2,1,0:T(8,128)S(1)}, f32[2,2,32,1024]{3,2,1,0:T(8,128)}, u32[]{:S(2)}) copy-start(f32[2,2,32,1024]{3,2,1,0:T(8,128)} %param.10) | copy-start | bytes 1572868
  240.5 5.8 %collective-permute-start.2 = (f32[2,32,1024]{2,1,0:T(8,128)S(1)}, f32[2,32,1024]{2,1,0:T(8,128)S(1)}, u32[]{:S(2)}, u32[]{:S(2)}) collective-permute-start(f32[2,32,1024]{2,1,0:T(8,128)S(1)} %pad_maximum_fusion.5), channel_id=1, source_target_pairs={{16,0},{32,16},{48,32},{64,48},{80,64},{96,80},{112,96},{17,1},{33... | collective-permute-start | bytes 786440 | tf_op jit(solution)/shard_map/ppermute | solution.py:12
  246.9 33.4 %copy-start.21 = (bf16[1,1024,1024]{2,1,0:T(8,128)(2,1)S(1)}, bf16[1,1024,1024]{2,1,0:T(8,128)(2,1)}, u32[]{:S(2)}) copy-start(bf16[1,1024,1024]{2,1,0:T(8,128)(2,1)} %param.11) | copy-start | bytes 6291460
  280.3 1.3 copy-start.1
  281.6 2.4 copy-start.8
  284.0 1.5 copy-start.10
  289.2 71.4 %all-to-all-start.5 = ((f32[16,32,2048]{2,1,0:T(8,128)}), f32[16,32,2048]{2,1,0:T(8,128)}, u32[]{:S(2)}, u32[]{:S(2)}) async-start(f32[16,32,2048]{2,1,0:T(8,128)} %bitcast.142), calls=%async_computation.5 | async-start | bytes 8388608 | tf_op jit(solution)/shard_map/all_to_all | solution.py:46
  294.0 3.0 copy-start.4
  294.0 3.0 copy-start.23
  297.1 1.6 copy-start.6
  297.1 1.8 copy-start.14
  298.9 1.6 copy-start.25
  300.5 1.6 copy-start.2
  300.5 1.9 copy-start.11
  302.4 3.4 copy-start.9
  (1 other events, 1.3 us)
where the time goes:
time: 366 us; the launch traced here: 365 us
  waiting for transfers between devices  177 us (48%)
  blocking collectives  103 us (28%)
  matrix products  33.3 us (9%)
  other arithmetic  23.9 us (7%)
  starting transfers between devices  21.8 us (6%)
  local copies, waits for them, and re-layouts  5.04 us (1%)
    all_to_all x3, waiting for transfers between devices, sent_and_summed(): lax.all_to_all(in_blocks(array, dim, devices), axis, 0, 0, tiled=True)  170 us
    all_to_all x3, blocking collectives, sent_to_all(): return lax.all_to_all(copies, axis, split_axis=0, concat_axis=0, tiled=True)  103 us
    all_to_all x3, starting transfers between devices, sent_and_summed(): lax.all_to_all(in_blocks(array, dim, devices), axis, 0, 0, tiled=True)  14 us
    ppermute x4, starting transfers between devices, from_behind(): lax.ppermute(value, axis, [(source, source + steps) for source in range(i...  7.78 us
    dot_general x3, matrix products, shards(): jnp.dot(full_lift.T, back_pre, preferred_element_type=jnp.float32)  7.66 us
    concatenate x3, other arithmetic, shards(): jnp.concatenate([jnp.dot(hidden, weight_out, preferred_element_type=jnp.f...  7.5 us
  transfers between devices with their start and end apart: 7, of which 5 were waited for; matrix products, arithmetic and copies ran while one was open for 7% of the time, Pallas kernels for 0%

commit v1 on v0

v1 whole, which is shorter than its diff:
```python
from functools import partial

import jax
import jax.numpy as jnp
from jax import lax
from jax.experimental import pallas as pl
from jax.experimental.pallas import tpu as pltpu
from jax.sharding import PartitionSpec as P

MESH = pl.DeviceIdType.MESH
BF = jnp.bfloat16
F32 = jnp.float32
CHUNKS = 2
SIDE = 4
TILE = 256
N_COPY = 48
GELU_A = 0.044715
GELU_C = 0.7978845608028654


def dot_nn(a, b):
    return lax.dot_general(a, b, (((1,), (0,)), ((), ())), preferred_element_type=F32)


def dot_nt(a, b):
    return lax.dot_general(a, b, (((1,), (1,)), ((), ())), preferred_element_type=F32)


def dot_tn(a, b):
    return lax.dot_general(a, b, (((0,), (0,)), ((), ())), preferred_element_type=F32)


def kernel(
    streams, cots, feed_s, feed_c, w_in_hbm, w_out_hbm, gain_hbm,
    out_s, out_c, out_gin, out_gout,
    st, ct, fs, fc, w_in, w_out, gain,
    held, got, shift,
    ga, gb, hid, bpre, pa, pb,
    big_f, big_d, big_e, big_c, summed, summed_b, small_f, small_d, small_e, small_c,
    acc_in, acc_out,
    ssem, rsem, lsem,
):
    ticks = feed_s.shape[0] + 1
    rows, width = st.shape[1], st.shape[2]
    r = rows // CHUNKS
    half = width // 2
    sections = lax.axis_size("section")
    sec = lax.axis_index("section")
    h = lax.axis_index("hid")
    x, z = lax.rem(h, SIDE), lax.div(h, SIDE)
    top = sec == sections - 1

    def wrap(v, by):
        return lax.rem(v + (by + SIDE), SIDE)

    def along_x(by):
        return {"hid": z * SIDE + wrap(x, by)}

    def along_z(by):
        return {"hid": wrap(z, by) * SIDE + x}

    below = {"section": lax.rem(sec + sections - 1, sections)}
    above = {"section": lax.rem(sec + 1, sections)}

    loads = []

    def load(i, src, dst):
        copy = pltpu.make_async_copy(src, dst, lsem.at[i])
        copy.start()
        return copy

    first_loads = [load(0, streams.at[0], st), load(1, cots.at[0], ct), load(2, gain_hbm, gain)]
    weight_loads = [load(3, w_in_hbm.at[0], w_in), load(4, w_out_hbm.at[0], w_out)]
    feed_loads = [load(5, feed_s, fs), load(6, feed_c, fc)]

    barrier = pltpu.get_barrier_semaphore()
    for peer in (along_x(1), along_x(-1), along_z(1), along_z(-1), above, below):
        pl.semaphore_signal(barrier, inc=1, device_id=peer, device_id_type=MESH)
    pl.semaphore_wait(barrier, 6)
    for copy in first_loads:
        copy.wait()

    class Lane:
        def __init__(self, q, which):
            self.q, self.which = q, which
            if which == 0:
                self.m, self.big = x, z
                self.small_dev, self.big_dev = along_x, along_z
                self.g, self.p = ga.at[q], pa.at[q]
            else:
                self.m, self.big = z, x
                self.small_dev, self.big_dev = along_z, along_x
                self.g, self.p = gb.at[q], pb.at[q]
            self.base = which * 22

        def single(self, ref, big, m):
            return ref.at[big, m] if self.which == 0 else ref.at[m, big]

        def pair(self, ref, big, part):
            two = pl.ds(2 * part, 2)
            return ref.at[big, two] if self.which == 0 else ref.at[two, big]

        def copy(self, i, src, dst, dev):
            return pltpu.make_async_remote_copy(
                src_ref=src, dst_ref=dst,
                send_sem=ssem.at[self.q, self.base + i], recv_sem=rsem.at[self.q, self.base + i],
                device_id=dev, device_id_type=MESH,
            )

        def send(self, i, src, dst, dev):
            self.copy(i, src, dst, dev).start()
            waits.append((self.q, self.base + i, src))

        def arrived(self, i, dst):
            self.copy(i, dst, dst, self.small_dev(1)).wait_recv()

        def a0(self):
            own = self.single(self.g, self.big, self.m)
            self.send(0, own, own, self.small_dev(1))
            self.send(1, own, own, self.small_dev(-1))

        def a1(self):
            lower = self.single(self.g, self.big, wrap(self.m, -1))
            upper = self.single(self.g, self.big, wrap(self.m, 1))
            self.arrived(0, lower)
            left = lower.at[:, pl.ds(0, half)]
            self.send(2, left, left, self.small_dev(1))
            self.arrived(1, upper)
            right = upper.at[:, pl.ds(half, half)]
            self.send(3, right, right, self.small_dev(-1))

        def a2(self):
            far = self.single(self.g, self.big, wrap(self.m, 2))
            self.arrived(2, far.at[:, pl.ds(0, half)])
            self.arrived(3, far.at[:, pl.ds(half, half)])
            one, two = self.pair(self.g, self.big, 0), self.pair(self.g, self.big, 1)
            self.send(4, one, one, self.big_dev(1))
            self.send(5, two, two, self.big_dev(-1))
            self.send(6, two, two, self.big_dev(1))
            self.send(7, one, one, self.big_dev(-1))

        def a3(self):
            one = self.pair(self.g, wrap(self.big, -1), 0)
            two = self.pair(self.g, wrap(self.big, 1), 1)
            self.arrived(4, one)
            self.send(8, one, one, self.big_dev(1))
            self.arrived(5, two)
            self.send(9, two, two, self.big_dev(-1))

        def a4(self):
            self.arrived(6, self.pair(self.g, wrap(self.big, -1), 1))
            self.arrived(7, self.pair(self.g, wrap(self.big, 1), 0))
            self.arrived(8, self.pair(self.g, wrap(self.big, 2), 0))
            self.arrived(9, self.pair(self.g, wrap(self.big, 2), 1))

        def slot(self, ref, i):
            return ref.at[self.q, self.which, i]

        def r0(self):
            p = self.p
            up, down, far = wrap(self.big, 1), wrap(self.big, -1), wrap(self.big, 2)
            self.send(10, self.pair(p, far, 0), self.slot(big_f, 0), self.big_dev(1))
            self.send(11, self.pair(p, far, 1), self.slot(big_f, 1), self.big_dev(-1))
            self.send(12, self.pair(p, up, 1), self.slot(big_d, 0), self.big_dev(1))
            self.send(13, self.pair(p, down, 0), self.slot(big_d, 1), self.big_dev(-1))

        def r1(self):
            for i, by in ((0, 1), (1, -1)):
                arrived, both = self.slot(big_f, i), self.slot(big_c, i)
                self.arrived(10 + i, arrived)
                own = self.pair(self.p, wrap(self.big, by), i)[...]
                both[...] = (own.astype(F32) + arrived[...].astype(F32)).astype(BF)
                self.send(14 + i, both, self.slot(big_e, i), self.big_dev(by))

        def r2(self):
            for i in (0, 1):
                self.arrived(12 + i, self.slot(big_d, i))
                self.arrived(14 + i, self.slot(big_e, i))
            total, total_b = summed.at[self.q % CHUNKS, self.which], summed_b.at[self.q, self.which]
            for part in (0, 1):
                value = (
                    self.pair(self.p, self.big, part)[...].astype(F32)
                    + self.slot(big_e, part)[...].astype(F32)
                    + self.slot(big_d, 1 - part)[...].astype(F32)
                )
                total[pl.ds(2 * part, 2)] = value
                total_b[pl.ds(2 * part, 2)] = value.astype(BF)
            up, down, far = wrap(self.m, 1), wrap(self.m, -1), wrap(self.m, 2)
            left, right = pl.ds(0, half), pl.ds(half, half)
            self.send(16, total_b.at[far, :, left], self.slot(small_f, 0), self.small_dev(1))
            self.send(17, total_b.at[far, :, right], self.slot(small_f, 1), self.small_dev(-1))
            self.send(18, total_b.at[up, :, right], self.slot(small_d, 0), self.small_dev(1))
            self.send(19, total_b.at[down, :, left], self.slot(small_d, 1), self.small_dev(-1))

        def r3(self):
            total = summed.at[self.q % CHUNKS, self.which]
            for i, by in ((0, 1), (1, -1)):
                arrived, both = self.slot(small_f, i), self.slot(small_c, i)
                self.arrived(16 + i, arrived)
                own = total[wrap(self.m, by), :, pl.ds(i * half, half)]
                both[...] = (own + arrived[...].astype(F32)).astype(BF)
                self.send(20 + i, both, self.slot(small_e, i), self.small_dev(by))

        def r4(self):
            total = summed.at[self.q % CHUNKS, self.which]
            for i in (0, 1):
                self.arrived(18 + i, self.slot(small_d, i))
                self.arrived(20 + i, self.slot(small_e, i))
            parts = [
                total[self.m, :, pl.ds(i * half, half)]
                + self.slot(small_e, i)[...].astype(F32)
                + self.slot(small_d, 1 - i)[...].astype(F32)
                for i in (0, 1)
            ]
            return jnp.concatenate(parts, axis=-1)

    waits = []
    out_copies = []

    def pass_on(q, i, src, dst):
        copy = pltpu.make_async_remote_copy(
            src_ref=src, dst_ref=dst, send_sem=ssem.at[q, 44 + i], recv_sem=rsem.at[q, 44 + i],
            device_id=below, device_id_type=MESH,
        )
        copy.start()
        waits.append((q, 44 + i, src))

    def normalized(first):
        scale_row = lax.rsqrt(jnp.mean(first * first, axis=-1, keepdims=True) + 1e-06)
        return first * scale_row, scale_row

    class Chunk:
        def __init__(self, t, c):
            self.t, self.c, self.q = t, c, t * CHUNKS + c
            self.rows = pl.ds(c * r, r)
            self.lanes = (Lane(self.q, 0), Lane(self.q, 1))

        def start(self):
            t, q = self.t, self.q
            mine = held.at[q]
            if t == 0:
                mine[0], mine[1] = st[0, self.rows], st[1, self.rows]
                mine[2], mine[3] = ct[0, self.rows], ct[1, self.rows]
            else:
                before = q - CHUNKS
                came = got.at[before]
                for i, place in ((0, 1), (1, 2), (2, 0), (3, 3)):
                    pltpu.make_async_remote_copy(
                        src_ref=came.at[place], dst_ref=came.at[place],
                        send_sem=ssem.at[before, 44 + i], recv_sem=rsem.at[before, 44 + i],
                        device_id=below, device_id_type=MESH,
                    ).wait_recv()
                for i, (feed, part) in enumerate(((fs, 0), (fs, 1), (fc, 0), (fc, 1))):
                    mine[i] = jnp.where(top, feed[t - 1, part, self.rows], came[i])
            normed, _ = normalized(mine[0])
            ga[q, z, x] = (normed * gain[...]).astype(BF)
            gb[q, z, x] = mine[3].astype(BF)
            for lane in self.lanes:
                lane.a0()
            if t < ticks - 1:
                pass_on(q, 0, mine.at[0], got.at[q, 1])
                pass_on(q, 1, mine.at[3], got.at[q, 2])

        def step(self, name):
            for lane in self.lanes:
                getattr(lane, name)()

        def k1(self):
            q = self.q
            n = SIDE * SIDE * r

            def body(j, carry):
                cols = pl.ds(pl.multiple_of(j * TILE, TILE), TILE)
                pre = dot_nn(ga[q].reshape(n, width), w_in[:, cols])
                back = dot_nt(gb[q].reshape(n, width), w_out[cols, :])
                sq = pre * pre
                th = jnp.tanh(pre * (GELU_C + (GELU_C * GELU_A) * sq))
                cdf = 0.5 + 0.5 * th
                slope = cdf + (0.5 * pre) * (1.0 - th * th) * (GELU_C + (3.0 * GELU_C * GELU_A) * sq)
                hid[q, :, cols] = (pre * cdf).astype(BF)
                bpre[q, :, cols] = (back * slope).astype(BF)
                return carry

            lax.fori_loop(0, w_in.shape[1] // TILE, body, 0)

        def k2(self):
            q = self.q

            def body(j, carry):
                cols = pl.ds(pl.multiple_of(j * TILE, TILE), TILE)
                out = dot_nn(hid[q], w_out[:, cols])
                pa[q, :, :, :, cols] = out.astype(BF).reshape(SIDE, SIDE, r, TILE)
                lift = dot_nt(bpre[q], w_in[cols, :])
                pb[q, :, :, :, cols] = lift.astype(BF).reshape(SIDE, SIDE, r, TILE)
                return carry

            lax.fori_loop(0, width // TILE, body, 0)

        def finish(self):
            t, q = self.t, self.q
            mine = held.at[q]
            block_out = self.lanes[0].r4()
            back_lift = self.lanes[1].r4()
            normed, scale_row = normalized(mine[0])
            back_norm = back_lift * gain[...]
            shift[q, 0] = mine[1] - block_out
            shift[q, 1] = mine[2] + scale_row * (
                back_norm - normed * jnp.mean(back_norm * normed, axis=-1, keepdims=True)
            )
            if t < ticks - 1:
                pass_on(q, 2, shift.at[q, 0], got.at[q, 0])
                pass_on(q, 3, shift.at[q, 1], got.at[q, 3])
            else:
                for i, (src, dst, part) in enumerate((
                    (shift.at[q, 0], out_s, 0), (mine.at[0], out_s, 1),
                    (mine.at[3], out_c, 0), (shift.at[q, 1], out_c, 1),
                )):
                    out_copies.append(load(7 + 4 * self.c + i, src, dst.at[0, part, self.rows]))

    pieces = []

    def weight_piece(t, which, lo, count):
        left, right, acc, out = (
            (ga, bpre, acc_in, out_gin) if which == 0 else (hid, gb, acc_out, out_gout)
        )
        n = SIDE * SIDE * r

        def whole(ref, cols):
            if ref is ga or ref is gb:
                parts = [ref[t * CHUNKS + c, :, :, :, cols].reshape(n, -1) for c in range(CHUNKS)]
            else:
                parts = [ref[t * CHUNKS + c, :, cols] for c in range(CHUNKS)]
            return jnp.concatenate(parts, axis=0)

        def body(j, carry):
            cols = pl.ds(pl.multiple_of(j * TILE, TILE), TILE)
            part = dot_tn(whole(left, cols), whole(right, pl.ds(0, width)))
            acc[cols, :] = part if t == 0 else acc[cols, :] + part
            return carry

        lax.fori_loop(lo, lo + count, body, 0)
        if t == ticks - 1:
            span = pl.ds(lo * TILE, count * TILE)
            out_copies.append(load(16 + 4 * which + lo, acc.at[span], out.at[0, span]))

    def fill(count):
        for _ in range(count):
            if pieces:
                weight_piece(*pieces.pop(0))

    def ready(t):
        for which in (0, 1):
            for lo in (0, 2):
                pieces.append((t, which, lo, 2))

    prev = None
    for t in range(ticks):
        c0, c1 = Chunk(t, 0), Chunk(t, 1)
        c0.start()
        if prev:
            prev.step("r1")
        c0.step("a1")
        if prev:
            prev.step("r2")
        c0.step("a2")
        if prev:
            prev.step("r3")
            fill(1)
        c0.step("a3")
        if prev:
            prev.finish()
            fill(1)
        if t == 0:
            for copy in weight_loads + feed_loads:
                copy.wait()
        if not prev:
            c1.start()
        c0.step("a4")
        if not prev:
            c1.step("a1")
        c0.k1()
        if prev:
            c1.start()
        else:
            c1.step("a2")
        c0.k2()
        c0.step("r0")
        if prev:
            c1.step("a1")
            c1.step("a2")
        c0.step("r1")
        c1.step("a3")
        c0.step("r2")
        c1.step("a4")
        c0.step("r3")
        c1.k1()
        c0.finish()
        c1.k2()
        c1.step("r0")
        ready(t)
        fill(2)
        prev = c1
    prev.step("r1")
    fill(1)
    prev.step("r2")
    fill(1)
    prev.step("r3")
    fill(2)
    prev.finish()
    fill(len(pieces))
    for copy in out_copies:
        copy.wait()
    for q, i, src in waits:
        pltpu.make_async_remote_copy(
            src_ref=src, dst_ref=src, send_sem=ssem.at[q, i], recv_sem=rsem.at[q, i],
            device_id=below, device_id_type=MESH,
        ).wait_send()


def shards(streams, cotangents, feed_streams, feed_cotangents, w_in, w_out, gain):
    ticks = feed_streams.shape[0] + 1
    rows, width = streams.shape[2], streams.shape[3]
    hidden = w_in.shape[2]
    r = rows // CHUNKS
    n = SIDE * SIDE * r
    q = ticks * CHUNKS
    blocks = (q, SIDE, SIDE, r, width)
    hbm = pl.BlockSpec(memory_space=pl.ANY)
    half = width // 2
    return pl.pallas_call(
        kernel,
        out_shape=(
            jax.ShapeDtypeStruct(streams.shape, F32),
            jax.ShapeDtypeStruct(cotangents.shape, F32),
            jax.ShapeDtypeStruct(w_in.shape, F32),
            jax.ShapeDtypeStruct(w_out.shape, F32),
        ),
        in_specs=[hbm] * 7,
        out_specs=(hbm,) * 4,
        scratch_shapes=[
            pltpu.VMEM((2, rows, width), F32),
            pltpu.VMEM((2, rows, width), F32),
            pltpu.VMEM(feed_streams.shape, F32),
            pltpu.VMEM(feed_cotangents.shape, F32),
            pltpu.VMEM((width, hidden), BF),
            pltpu.VMEM((hidden, width), BF),
            pltpu.VMEM((1, width), F32),
            pltpu.VMEM((q, 4, r, width), F32),
            pltpu.VMEM((q - CHUNKS, 4, r, width), F32),
            pltpu.VMEM((q, 2, r, width), F32),
            pltpu.VMEM(blocks, BF),
            pltpu.VMEM(blocks, BF),
            pltpu.VMEM((q, n, hidden), BF),
            pltpu.VMEM((q, n, hidden), BF),
            pltpu.VMEM(blocks, BF),
            pltpu.VMEM(blocks, BF),
            pltpu.VMEM((q, 2, 2, 2, r, width), BF),
            pltpu.VMEM((q, 2, 2, 2, r, width), BF),
            pltpu.VMEM((q, 2, 2, 2, r, width), BF),
            pltpu.VMEM((q, 2, 2, 2, r, width), BF),
            pltpu.VMEM((CHUNKS, 2, SIDE, r, width), F32),
            pltpu.VMEM((q, 2, SIDE, r, width), BF),
            pltpu.VMEM((q, 2, 2, r, half), BF),
            pltpu.VMEM((q, 2, 2, r, half), BF),
            pltpu.VMEM((q, 2, 2, r, half), BF),
            pltpu.VMEM((q, 2, 2, r, half), BF),
            pltpu.VMEM((width, hidden), F32),
            pltpu.VMEM((hidden, width), F32),
            pltpu.SemaphoreType.DMA((q, N_COPY)),
            pltpu.SemaphoreType.DMA((q, N_COPY)),
            pltpu.SemaphoreType.DMA((24,)),
        ],
        compiler_params=pltpu.CompilerParams(
            collective_id=0, has_side_effects=True, vmem_limit_bytes=60 * 1024 * 1024
        ),
    )(streams, cotangents, feed_streams, feed_cotangents, w_in, w_out, gain)


def solution(mesh):
    placed = (
        P("section", None, "hid", None),
        P("section", None, "hid", None),
        P(None, None, "hid", None),
        P(None, None, "hid", None),
        P("section", None, "hid"),
        P("section", "hid", None),
        P("section", None),
    )
    return jax.shard_map(
        shards,
        mesh=mesh,
        in_specs=placed,
        out_specs=(
            P("section", None, "hid", None),
            P("section", None, "hid", None),
            P("section", None, "hid"),
            P("section", "hid", None),
        ),
        check_vma=False,
    )
```

time: 366 us -> 162 us (0.44)
  waiting for transfers between devices: 177 us -> 0 us
  Pallas kernels: 0 us -> 151 us
  blocking collectives: 103 us -> 0 us
  matrix products: 33.3 us -> 0 us
  other arithmetic: 23.9 us -> 0 us
  starting transfers between devices: 21.8 us -> 0 us
  local copies, waits for them, and re-layouts: 5.04 us -> 10.3 us
    all_to_all x3 -> x0, waiting for transfers between devices: 170 us -> none  [sent_and_summed(): lax.all_to_all(in_blocks(array, dim, devices), axis, 0, 0, tiled=True)]
    pallas_call x0 -> x1, Pallas kernels: none -> 151 us  [shards(): pl.pallas_call(kernel, out_shape=(jax.ShapeDtypeStruct(streams.shape, F32...]
    all_to_all x3 -> x0, blocking collectives: 103 us -> none  [sent_to_all(): return lax.all_to_all(copies, axis, split_axis=0, concat_axis=0, tiled=True)]
    dot_general x18 -> x0, matrix products: 33.3 us -> none  [the longest x3 7.66 us: shards(): jnp.dot(full_lift.T, back_pre, preferred_element_type=jnp.float32)]
    all_to_all x3 -> x0, starting transfers between devices: 14 us -> none  [sent_and_summed(): lax.all_to_all(in_blocks(array, dim, devices), axis, 0, 0, tiled=True)]
    reduce_sum x9 -> x0, other arithmetic: 9.23 us -> none  [the longest x3 7.25 us: sent_and_summed(): return jnp.sum(blocks, axis=0)]
    unnamed x52 -> x6, local copies, waits for them, and re-layouts: 1.29 us -> 10.3 us
    ppermute x4 -> x0, starting transfers between devices: 7.78 us -> none  [from_behind(): lax.ppermute(value, axis, [(source, source + steps) for source in range(i...]
  transfers between devices with their start and end apart: 7 -> 0, of which waited for: 5 -> 0; matrix products, arithmetic and copies ran while one was open for 7% -> 0% of each run, Pallas kernels for 0% -> 0%
where the time goes in v1:
time: 162 us
  Pallas kernels  151 us (93%)
  local copies, waits for them, and re-layouts  10.3 us (6%)
    pallas_call x1, Pallas kernels, shards(): pl.pallas_call(kernel, out_shape=(jax.ShapeDtypeStruct(streams.shape, F32...  151 us
    unnamed x6, local copies, waits for them, and re-layouts  10.3 us

profile of v1, /device:TPU:8, one launch (start us, length us, event | category | flops | bytes accessed | tf_op | source)
XLA Modules:
  0.0 162.2 jit_solution(238032966511556640)
XLA Ops:
  0.6 151.3 %shard_map.102 = (f32[1,2,32,1024]{3,2,1,0:T(8,128)}, f32[1,2,32,1024]{3,2,1,0:T(8,128)}, f32[1,1024,1024]{2,1,0:T(8,128)}, f32[1,1024,1024]{2,1,0:T(8,128)}) custom-call(f32[1,2,32,1024]{3,2,1,0:T(8,128)} %streams.1, f32[1,2,32,1024]{3,2,1,0:T(8,128)} %cots.1, f32[2,2,32,1024]{3,2,1,0:T(8,128)} %feed_s.1, f32[2,2,32,1024]{3,2,1,0:T(8,128)} %feed_c.1, ...), custom_call_target="tpu_custom_call" | custom-call | tf_op jit(solution)/shard_map/pallas_call | solution.py:430
  151.9 1.7 %copy.15 = f32[1,2,32,1024]{3,2,1,0:T(8,128)} copy(f32[1,2,32,1024]{3,2,1,0:T(8,128)} %get-tuple-element.8) | data formatting | bytes 524288
  153.6 1.7 %copy.16 = f32[1,2,32,1024]{3,2,1,0:T(8,128)} copy(f32[1,2,32,1024]{3,2,1,0:T(8,128)} %get-tuple-element.9) | data formatting | bytes 524288
  155.3 0.0 copy-start
  155.3 4.9 %copy.17 = f32[1,1024,1024]{2,1,0:T(8,128)} copy(f32[1,1024,1024]{2,1,0:T(8,128)} %get-tuple-element.10) | data formatting | bytes 8388608
  160.2 0.0 copy-done
  160.2 2.0 %copy.18 = f32[1,1024,1024]{2,1,0:T(8,128)} copy(f32[1,1024,1024]{2,1,0:T(8,128)S(1)} %copy-done) | data formatting | bytes 8388608
Async XLA Ops:
  155.3 4.9 %copy-start = (f32[1,1024,1024]{2,1,0:T(8,128)S(1)}, f32[1,1024,1024]{2,1,0:T(8,128)}, u32[]{:S(2)}) copy-start(f32[1,1024,1024]{2,1,0:T(8,128)} %get-tuple-element.11) | copy-start | bytes 12582916

commit v2 on v0

v2 whole, which is shorter than its diff:
```python
from functools import partial

import jax
import jax.numpy as jnp
from jax import lax
from jax.experimental import pallas as pl
from jax.experimental.pallas import tpu as pltpu
from jax.sharding import PartitionSpec as P

MESH = pl.DeviceIdType.MESH
BF = jnp.bfloat16
F32 = jnp.float32
CHUNKS = 2
SIDE = 4
TILE = 1024
GRAD_TILE = 256
STEPS = (2, 1, -1)
LANE_COPIES = 19
RELAY_GATHER = False
RELAY_SUM = False
PASS = 2 * LANE_COPIES
N_COPY = PASS + 3
GELU_A = 0.044715
GELU_C = 0.7978845608028654


def dot_nn(a, b):
    return lax.dot_general(a, b, (((1,), (0,)), ((), ())), preferred_element_type=F32)


def dot_nt(a, b):
    return lax.dot_general(a, b, (((1,), (1,)), ((), ())), preferred_element_type=F32)


def dot_tn(a, b):
    return lax.dot_general(a, b, (((0,), (0,)), ((), ())), preferred_element_type=F32)


ORDER = (
    (0, 0, 0, "S"), (0, 0, 1, "S"), (0, 1, 0, "S"), (0, 1, 1, "S"), (0, 0, 0, "a2"), (0, 0, 1, "a2"),
    (0, 1, 0, "a2"), (0, 1, 1, "a2"), (0, 0, 0, "a4"), (0, 0, 0, "K1"), (0, 0, 0, "K2"), (0, 0, 0, "r0"),
    (0, 0, 1, "a4"), (0, 0, 1, "K1"), (0, 0, 1, "K2"), (0, 0, 1, "r0"), (0, 1, 0, "a4"), (0, 1, 0, "K1"),
    (0, 1, 0, "K2"), (0, 1, 0, "r0"), (0, 1, 1, "a4"), (0, 1, 1, "K1"), (0, 1, 1, "K2"), (0, 1, 1, "r0"),
    (0, 0, 0, "r2"), (0, 0, 0, "W"), (0, 0, 2, "W"), (0, 0, 1, "r2"), (0, 1, 0, "W"), (0, 1, 2, "W"),
    (0, 1, 0, "r2"), (0, 1, 1, "r2"), (1, 0, 0, "S"), (1, 0, 1, "S"), (1, 1, 0, "S"), (1, 1, 1, "S"),
    (1, 0, 0, "a2"), (1, 0, 1, "a2"), (1, 1, 0, "a2"), (1, 1, 1, "a2"), (1, 0, 0, "a4"), (1, 0, 0, "K1"),
    (1, 0, 0, "K2"), (1, 0, 0, "r0"), (1, 0, 1, "a4"), (1, 0, 1, "K1"), (1, 0, 1, "K2"), (1, 0, 1, "r0"),
    (1, 1, 0, "a4"), (1, 1, 0, "K1"), (1, 1, 0, "K2"), (1, 1, 0, "r0"), (1, 1, 1, "a4"), (1, 1, 1, "K1"),
    (1, 1, 1, "K2"), (1, 1, 1, "r0"), (1, 0, 0, "r2"), (1, 0, 0, "W"), (1, 0, 2, "W"), (1, 0, 1, "r2"),
    (1, 1, 0, "W"), (1, 1, 2, "W"), (1, 1, 0, "r2"), (1, 1, 1, "r2"), (2, 0, 0, "S"), (2, 0, 1, "S"),
    (2, 1, 0, "S"), (2, 1, 1, "S"), (2, 0, 0, "a2"), (2, 0, 1, "a2"), (2, 1, 0, "a2"), (2, 1, 1, "a2"),
    (2, 0, 0, "a4"), (2, 0, 0, "K1"), (2, 0, 0, "K2"), (2, 0, 0, "r0"), (2, 0, 1, "a4"), (2, 0, 1, "K1"),
    (2, 0, 1, "K2"), (2, 0, 1, "r0"), (2, 1, 0, "a4"), (2, 1, 0, "K1"), (2, 1, 0, "K2"), (2, 1, 0, "r0"),
    (2, 1, 1, "a4"), (2, 1, 1, "K1"), (2, 1, 1, "K2"), (2, 1, 1, "r0"), (2, 0, 0, "r2"), (2, 0, 0, "W"),
    (2, 0, 2, "W"), (2, 0, 1, "r2"), (2, 1, 0, "W"), (2, 1, 2, "W"), (2, 1, 0, "r2"), (2, 0, 1, "F"),
    (2, 1, 1, "r2"), (2, 0, 0, "F"), (2, 1, 0, "F"), (2, 1, 1, "F"),
)


def order(ticks):
    return ORDER


def kernel(
    streams, cots, feed_s, feed_c, w_in_hbm, w_out_hbm, gain_hbm,
    out_s, out_c, out_gin, out_gout,
    st, ct, fs, fc, w_in, w_out, gain, gain_above,
    held, got, ga, gb, hid, bpre, pa, pb,
    big_r, slope, summed, summed_b, small_r,
    ssem, rsem, lsem,
):
    ticks = feed_s.shape[0] + 1
    rows, width = st.shape[1], st.shape[2]
    r = rows // CHUNKS
    n = SIDE * SIDE * r
    sections = lax.axis_size("section")
    sec = lax.axis_index("section")
    h = lax.axis_index("hid")
    x, z = lax.rem(h, SIDE), lax.div(h, SIDE)
    top = sec == sections - 1
    below = lax.rem(sec + sections - 1, sections)
    above = lax.rem(sec + 1, sections)

    def wrap(v, by):
        return lax.rem(v + (by + SIDE), SIDE)

    def along_x(by, section=sec):
        return {"section": section, "hid": z * SIDE + wrap(x, by)}

    def along_z(by, section=sec):
        return {"section": section, "hid": wrap(z, by) * SIDE + x}

    def load(i, src, dst):
        copy = pltpu.make_async_copy(src, dst, lsem.at[i])
        copy.start()
        return copy

    first_loads = [load(0, streams.at[0], st), load(1, cots.at[0], ct), load(2, gain_hbm, gain)]
    weight_loads = [load(3, w_in_hbm.at[0], w_in), load(4, w_out_hbm.at[0], w_out)]
    feed_loads = [load(5, feed_s, fs), load(6, feed_c, fc)]

    barrier = pltpu.get_barrier_semaphore()
    peers = [axis(by, s) for s in (sec, above, below) for axis in (along_x, along_z) for by in STEPS]
    peers += [along_x(0, above), along_x(0, below)]
    for peer in peers:
        pl.semaphore_signal(barrier, inc=1, device_id=peer, device_id_type=MESH)
    pl.semaphore_wait(barrier, len(peers))
    for copy in first_loads:
        copy.wait()

    waits = []

    def remote(q, i, src, dst, dev):
        return pltpu.make_async_remote_copy(
            src_ref=src, dst_ref=dst, send_sem=ssem.at[q, i], recv_sem=rsem.at[q, i],
            device_id=dev, device_id_type=MESH,
        )

    def send(q, i, src, dst, dev):
        remote(q, i, src, dst, dev).start()
        waits.append((q, i, src))

    def arrived(q, i, dst):
        remote(q, i, dst, dst, along_x(0, below)).wait_recv()

    class Lane:
        def __init__(self, t, q, which):
            self.t, self.q, self.which = t, q, which
            if which == 0:
                self.m, self.big = x, z
                self.small_dev, self.big_dev = along_x, along_z
                self.g, self.p = ga.at[q], pa.at[q]
            else:
                self.m, self.big = z, x
                self.small_dev, self.big_dev = along_z, along_x
                self.g, self.p = gb.at[q], pb.at[q]
            self.base = which * LANE_COPIES

        def single(self, ref, big, m):
            return ref.at[big, m] if self.which == 0 else ref.at[m, big]

        def group(self, ref, big):
            return ref.at[big] if self.which == 0 else ref.at[:, big]

        def pair(self, ref, big, part):
            two = pl.ds(2 * part, 2)
            return ref.at[big, two] if self.which == 0 else ref.at[two, big]

        def send(self, i, src, dst, dev):
            send(self.q, self.base + i, src, dst, dev)

        def arrived(self, i, dst):
            arrived(self.q, self.base + i, dst)

        def a0(self):
            own = self.single(self.g, self.big, self.m)
            for i, by in enumerate(STEPS):
                self.send(i, own, own, self.small_dev(by))

        def a2(self):
            for i, by in enumerate(STEPS):
                self.arrived(i, self.single(self.g, self.big, wrap(self.m, -by)))
            if RELAY_GATHER:
                one, two = self.pair(self.g, self.big, 0), self.pair(self.g, self.big, 1)
                self.send(3, one, one, self.big_dev(1))
                self.send(4, two, two, self.big_dev(-1))
                self.send(5, two, two, self.big_dev(1))
                self.send(6, one, one, self.big_dev(-1))
            else:
                mine = self.group(self.g, self.big)
                for i, by in enumerate(STEPS):
                    self.send(3 + i, mine, mine, self.big_dev(by))

        def a3(self):
            if RELAY_GATHER:
                one = self.pair(self.g, wrap(self.big, -1), 0)
                two = self.pair(self.g, wrap(self.big, 1), 1)
                self.arrived(3, one)
                self.send(7, one, one, self.big_dev(1))
                self.arrived(4, two)
                self.send(8, two, two, self.big_dev(-1))

        def a4(self):
            if RELAY_GATHER:
                self.arrived(5, self.pair(self.g, wrap(self.big, -1), 1))
                self.arrived(6, self.pair(self.g, wrap(self.big, 1), 0))
                self.arrived(7, self.pair(self.g, wrap(self.big, 2), 0))
                self.arrived(8, self.pair(self.g, wrap(self.big, 2), 1))
            else:
                for i, by in enumerate(STEPS):
                    self.arrived(3 + i, self.group(self.g, wrap(self.big, -by)))

        def slot(self, kind, i):
            return big_p.at[self.q, self.which, 2 * kind + i]

        def r0(self):
            if RELAY_SUM:
                up, down, far = wrap(self.big, 1), wrap(self.big, -1), wrap(self.big, 2)
                self.send(9, self.pair(self.p, far, 0), self.slot(0, 0), self.big_dev(1))
                self.send(10, self.pair(self.p, far, 1), self.slot(0, 1), self.big_dev(-1))
                self.send(11, self.pair(self.p, up, 1), self.slot(1, 0), self.big_dev(1))
                self.send(12, self.pair(self.p, down, 0), self.slot(1, 1), self.big_dev(-1))
            else:
                for i, by in enumerate(STEPS):
                    self.send(
                        9 + i, self.group(self.p, wrap(self.big, by)),
                        big_r.at[self.q, self.which, i], self.big_dev(by),
                    )

        def r1(self):
            if RELAY_SUM:
                for i, by in ((0, 1), (1, -1)):
                    came, both = self.slot(0, i), self.slot(3, i)
                    self.arrived(9 + i, came)
                    own = self.pair(self.p, wrap(self.big, by), i)[...]
                    both[...] = (own.astype(F32) + came[...].astype(F32)).astype(BF)
                    self.send(13 + i, both, self.slot(2, i), self.big_dev(by))

        def r2(self):
            last = self.t == ticks - 1
            total = summed_b.at[self.q, self.which]
            keep = summed.at[self.q % CHUNKS, self.which]
            if RELAY_SUM:
                for i in (0, 1):
                    self.arrived(11 + i, self.slot(1, i))
                    self.arrived(13 + i, self.slot(2, i))
                for part in (0, 1):
                    value = (
                        self.pair(self.p, self.big, part)[...].astype(F32)
                        + self.slot(2, part)[...].astype(F32)
                        + self.slot(1, 1 - part)[...].astype(F32)
                    )
                    if last:
                        keep[pl.ds(2 * part, 2)] = value
                    total[pl.ds(2 * part, 2)] = value.astype(BF)
            else:
                value = self.group(self.p, self.big)[...].astype(F32)
                for i in range(3):
                    self.arrived(9 + i, big_r.at[self.q, self.which, i])
                    value = value + big_r[self.q, self.which, i].astype(F32)
                if last:
                    keep[...] = value
                total[...] = value.astype(BF)
            for i, by in enumerate(STEPS if last else STEPS + (0,)):
                self.send(
                    15 + i, total.at[wrap(self.m, by)],
                    small_r.at[self.q, self.which, i], self.small_dev(by, sec if last else below),
                )

        def total(self):
            last = self.t == ticks - 1
            count = 3 if last else 4
            for i in range(count):
                self.arrived(15 + i, small_r.at[self.q, self.which, i])
            parts = [small_r[self.q, self.which, i].astype(F32) for i in range(count)]
            if last:
                parts.append(summed[self.q % CHUNKS, self.which, self.m])
            return (parts[0] + parts[1]) + (parts[2] + parts[3])

    def normalized(first):
        scale_row = lax.rsqrt(jnp.mean(first * first, axis=-1, keepdims=True) + 1e-06)
        return first * scale_row, scale_row

    def grad_of(first, grad_first, back_lift, gain_row):
        normed, scale_row = normalized(first)
        back_norm = back_lift * gain_row
        back = back_norm - normed * jnp.mean(back_norm * normed, axis=-1, keepdims=True)
        return grad_first + scale_row * back

    class Chunk:
        def __init__(self, t, c, before):
            self.t, self.c, self.q, self.before = t, c, t * CHUNKS + c, before
            self.rows = pl.ds(c * r, r)
            self.lanes = (Lane(t, self.q, 0), Lane(t, self.q, 1))

        def start(self, which):
            t, q = self.t, self.q
            mine = held.at[q]
            two = pl.ds(2 * which, 2)
            if t == 0:
                mine[two] = (ct if which else st)[:, self.rows]
            else:
                last_q = self.before.q
                came = got.at[last_q]
                arrived(last_q, PASS + which, came.at[two])
                total = self.before.lanes[which].total()
                if which == 0:
                    values = (came[1] - total, came[0])
                else:
                    values = (came[3], grad_of(came[0], came[2], total, gain_above[...]))
                feed = fc if which else fs
                for i in (0, 1):
                    mine[2 * which + i] = jnp.where(top, feed[t - 1, i, self.rows], values[i])
            if which == 0:
                ga[q, z, x] = (normalized(mine[0])[0] * gain[...]).astype(BF)
            else:
                gb[q, z, x] = mine[3].astype(BF)
            self.lanes[which].a0()
            if t < ticks - 1:
                send(q, PASS + which, mine.at[two], got.at[q, two], along_x(0, below))

        def finish(self, which):
            mine = held.at[self.q]
            total = self.lanes[which].total()
            if which == 0:
                out_s[0, 0, self.rows], out_s[0, 1, self.rows] = mine[1] - total, mine[0]
            else:
                out_c[0, 0, self.rows] = mine[3]
                out_c[0, 1, self.rows] = grad_of(mine[0], mine[2], total, gain[...])

        def tiles(self, body, size):
            def step(j, carry):
                body(pl.ds(pl.multiple_of(j * TILE, TILE), TILE))
                return carry

            lax.fori_loop(0, size // TILE, step, 0)

        def k1(self, which):
            q, c = self.q, self.c

            def lifted(cols):
                pre = dot_nn(ga[q].reshape(n, width), w_in[:, cols])
                sq = pre * pre
                th = jnp.tanh(pre * (GELU_C + (GELU_C * GELU_A) * sq))
                cdf = 0.5 + 0.5 * th
                hid[q, :, cols] = (pre * cdf).astype(BF)
                slope[c, :, cols] = cdf + (0.5 * pre) * (1.0 - th * th) * (
                    GELU_C + (3.0 * GELU_C * GELU_A) * sq
                )

            def cotan(cols):
                back = dot_nt(gb[q].reshape(n, width), w_out[cols, :])
                bpre[q, :, cols] = (back * slope[c, :, cols]).astype(BF)

            self.tiles(cotan if which else lifted, w_in.shape[1])

        def k2(self, which):
            q = self.q

            def block_out(cols):
                out = dot_nn(hid[q], w_out[:, cols])
                pa[q, :, :, :, cols] = out.astype(BF).reshape(SIDE, SIDE, r, TILE)

            def back_lift(cols):
                out = dot_nt(bpre[q], w_in[cols, :])
                pb[q, :, :, :, cols] = out.astype(BF).reshape(SIDE, SIDE, r, TILE)

            self.tiles(back_lift if which else block_out, width)

    def weight_piece(t, which, lo, count):
        left, right, acc = (ga, bpre, out_gin) if which == 0 else (hid, gb, out_gout)

        def whole(ref, cols):
            if ref is ga or ref is gb:
                parts = [ref[t * CHUNKS + c, :, :, :, cols].reshape(n, -1) for c in range(CHUNKS)]
            else:
                parts = [ref[t * CHUNKS + c, :, cols] for c in range(CHUNKS)]
            return jnp.concatenate(parts, axis=0)

        def body(j, carry):
            cols = pl.ds(pl.multiple_of(j * GRAD_TILE, GRAD_TILE), GRAD_TILE)
            part = dot_tn(whole(left, cols), whole(right, pl.ds(0, width)))
            acc[0, cols, :] = part if t == 0 else acc[0, cols, :] + part
            return carry

        lax.fori_loop(lo, lo + count, body, 0)

    chunks = {}
    for t in range(ticks):
        for c in range(CHUNKS):
            chunks[t, c] = Chunk(t, c, chunks.get((t - 1, c)))
    pending = {}

    def once(key, run):
        if key not in pending:
            pending[key] = True
            run()

    def wait_all(copies):
        for copy in copies:
            copy.wait()

    for t, c, which, what in order(ticks):
        if what == "W":
            weight_piece(t, c, which, 2)
            continue
        chunk = chunks[t, c]
        if what == "S":
            if t > 0:
                once("feed", lambda: wait_all(feed_loads))
                if which == 1:
                    once("gain", lambda: arrived(0, PASS + 2, gain_above))
            chunk.start(which)
            once("gain_sent", lambda: send(0, PASS + 2, gain, gain_above, along_x(0, below)))
        elif what == "F":
            chunk.finish(which)
        elif what == "K1":
            once("weights", lambda: wait_all(weight_loads))
            chunk.k1(which)
        elif what == "K2":
            chunk.k2(which)
        else:
            getattr(chunk.lanes[which], what)()
    for sent_q, i, src in waits:
        remote(sent_q, i, src, src, along_x(0, below)).wait_send()


def shards(streams, cotangents, feed_streams, feed_cotangents, w_in, w_out, gain):
    ticks = feed_streams.shape[0] + 1
    rows, width = streams.shape[2], streams.shape[3]
    hidden = w_in.shape[2]
    r = rows // CHUNKS
    n = SIDE * SIDE * r
    q = ticks * CHUNKS
    blocks = (q, SIDE, SIDE, r, width)
    hbm = pl.BlockSpec(memory_space=pltpu.HBM)
    vmem = pl.BlockSpec(memory_space=pltpu.VMEM)
    outs = (streams.shape, cotangents.shape, w_in.shape, w_out.shape)
    return pl.pallas_call(
        kernel,
        out_shape=tuple(pltpu.VMEM(s, F32) for s in outs),
        in_specs=[hbm] * 7,
        out_specs=(vmem,) * 4,
        scratch_shapes=[
            pltpu.VMEM((2, rows, width), F32),
            pltpu.VMEM((2, rows, width), F32),
            pltpu.VMEM(feed_streams.shape, F32),
            pltpu.VMEM(feed_cotangents.shape, F32),
            pltpu.VMEM((width, hidden), BF),
            pltpu.VMEM((hidden, width), BF),
            pltpu.VMEM((1, width), F32),
            pltpu.VMEM((1, width), F32),
            pltpu.VMEM((q, 4, r, width), F32),
            pltpu.VMEM((q - CHUNKS, 4, r, width), F32),
            pltpu.VMEM(blocks, BF),
            pltpu.VMEM(blocks, BF),
            pltpu.VMEM((q, n, hidden), BF),
            pltpu.VMEM((q, n, hidden), BF),
            pltpu.VMEM(blocks, BF),
            pltpu.VMEM(blocks, BF),
            pltpu.VMEM((q, 2, 3, SIDE, r, width), BF),
            pltpu.VMEM((CHUNKS, n, hidden), F32),
            pltpu.VMEM((CHUNKS, 2, SIDE, r, width), F32),
            pltpu.VMEM((q, 2, SIDE, r, width), BF),
            pltpu.VMEM((q, 2, 4, r, width), BF),
            pltpu.SemaphoreType.DMA((q, N_COPY)),
            pltpu.SemaphoreType.DMA((q, N_COPY)),
            pltpu.SemaphoreType.DMA((8,)),
        ],
        compiler_params=pltpu.CompilerParams(
            collective_id=0, has_side_effects=True, vmem_limit_bytes=50 * 1024 * 1024
        ),
    )(streams, cotangents, feed_streams, feed_cotangents, w_in, w_out, gain)


def solution(mesh):
    placed = (
        P("section", None, "hid", None),
        P("section", None, "hid", None),
        P(None, None, "hid", None),
        P(None, None, "hid", None),
        P("section", None, "hid"),
        P("section", "hid", None),
        P("section", None),
    )
    return jax.shard_map(
        shards,
        mesh=mesh,
        in_specs=placed,
        out_specs=(
            P("section", None, "hid", None),
            P("section", None, "hid", None),
            P("section", None, "hid"),
            P("section", "hid", None),
        ),
        check_vma=False,
    )
```

time: 366 us -> 118 us (0.32)
  waiting for transfers between devices: 177 us -> 0 us
  Pallas kernels: 0 us -> 111 us
  blocking collectives: 103 us -> 0 us
  matrix products: 33.3 us -> 0 us
  other arithmetic: 23.9 us -> 0 us
  starting transfers between devices: 21.8 us -> 0 us
    all_to_all x3 -> x0, waiting for transfers between devices: 170 us -> none  [sent_and_summed(): lax.all_to_all(in_blocks(array, dim, devices), axis, 0, 0, tiled=True)]
    pallas_call x0 -> x1, Pallas kernels: none -> 111 us  [shards(): pl.pallas_call(kernel, out_shape=tuple((pltpu.VMEM(s, F32) for s in outs)...]
    all_to_all x3 -> x0, blocking collectives: 103 us -> none  [sent_to_all(): return lax.all_to_all(copies, axis, split_axis=0, concat_axis=0, tiled=True)]
    dot_general x18 -> x0, matrix products: 33.3 us -> none  [the longest x3 7.66 us: shards(): jnp.dot(full_lift.T, back_pre, preferred_element_type=jnp.float32)]
    all_to_all x3 -> x0, starting transfers between devices: 14 us -> none  [sent_and_summed(): lax.all_to_all(in_blocks(array, dim, devices), axis, 0, 0, tiled=True)]
    reduce_sum x9 -> x0, other arithmetic: 9.23 us -> none  [the longest x3 7.25 us: sent_and_summed(): return jnp.sum(blocks, axis=0)]
    ppermute x4 -> x0, starting transfers between devices: 7.78 us -> none  [from_behind(): lax.ppermute(value, axis, [(source, source + steps) for source in range(i...]
    concatenate x6 -> x0, other arithmetic: 7.53 us -> none  [the longest x3 7.5 us: shards(): jnp.concatenate([jnp.dot(hidden, weight_out, preferred_element_type=jnp.f...]
  transfers between devices with their start and end apart: 7 -> 0, of which waited for: 5 -> 0; matrix products, arithmetic and copies ran while one was open for 7% -> 0% of each run, Pallas kernels for 0% -> 0%
where the time goes in v2:
time: 118 us; the launch traced here: 117 us
  Pallas kernels  111 us (94%)
  local copies, waits for them, and re-layouts  5.43 us (5%)
    pallas_call x1, Pallas kernels, shards(): pl.pallas_call(kernel, out_shape=tuple((pltpu.VMEM(s, F32) for s in outs)...  111 us
    unnamed x4, local copies, waits for them, and re-layouts  5.43 us

profile of v2, /device:TPU:8, one launch (start us, length us, event | category | flops | bytes accessed | tf_op | source)
XLA Modules:
  0.0 116.7 jit_solution(5813174485700340801)
XLA Ops:
  0.6 110.6 %shard_map.102 = (f32[1,2,32,1024]{3,2,1,0:T(8,128)S(1)}, f32[1,2,32,1024]{3,2,1,0:T(8,128)S(1)}, f32[1,1024,1024]{2,1,0:T(8,128)S(1)}, f32[1,1024,1024]{2,1,0:T(8,128)S(1)}) custom-call(f32[1,2,32,1024]{3,2,1,0:T(8,128)} %streams.1, f32[1,2,32,1024]{3,2,1,0:T(8,128)} %cots.1, f32[2,2,32,1024]{3,2,1,0:T(8,128)} %feed_s.1, f32[2,2,32,1024]{3,2,1,0:T(8,128)} %feed_c.1, ...), custom_call_target="tpu_custom_call" | custom-call | tf_op jit(solution)/shard_map/pallas_call | solution.py:419
  111.3 0.7 copy.15
  112.0 0.7 copy.16
  112.7 2.0 %copy.17 = f32[1,1024,1024]{2,1,0:T(8,128)} copy(f32[1,1024,1024]{2,1,0:T(8,128)S(1)} %get-tuple-element.6) | data formatting | bytes 8388608
  114.7 2.0 %copy.18 = f32[1,1024,1024]{2,1,0:T(8,128)} copy(f32[1,1024,1024]{2,1,0:T(8,128)S(1)} %get-tuple-element.7) | data formatting | bytes 8388608

commit v3 on v2

--- a/solution.py
+++ b/solution.py
@@ -13,11 +13,11 @@
 CHUNKS = 2
 SIDE = 4
 TILE = 1024
-GRAD_TILE = 256
+GRAD_TILE = 512
 STEPS = (2, 1, -1)
 LANE_COPIES = 19
-RELAY_GATHER = False
-RELAY_SUM = False
+RELAY_GATHER = True
+RELAY_SUM = True
 PASS = 2 * LANE_COPIES
 N_COPY = PASS + 3
 GELU_A = 0.044715
@@ -37,23 +37,27 @@
 
 
 ORDER = (
-    (0, 0, 0, "S"), (0, 0, 1, "S"), (0, 1, 0, "S"), (0, 1, 1, "S"), (0, 0, 0, "a2"), (0, 0, 1, "a2"),
-    (0, 1, 0, "a2"), (0, 1, 1, "a2"), (0, 0, 0, "a4"), (0, 0, 0, "K1"), (0, 0, 0, "K2"), (0, 0, 0, "r0"),
-    (0, 0, 1, "a4"), (0, 0, 1, "K1"), (0, 0, 1, "K2"), (0, 0, 1, "r0"), (0, 1, 0, "a4"), (0, 1, 0, "K1"),
-    (0, 1, 0, "K2"), (0, 1, 0, "r0"), (0, 1, 1, "a4"), (0, 1, 1, "K1"), (0, 1, 1, "K2"), (0, 1, 1, "r0"),
-    (0, 0, 0, "r2"), (0, 0, 0, "W"), (0, 0, 2, "W"), (0, 0, 1, "r2"), (0, 1, 0, "W"), (0, 1, 2, "W"),
-    (0, 1, 0, "r2"), (0, 1, 1, "r2"), (1, 0, 0, "S"), (1, 0, 1, "S"), (1, 1, 0, "S"), (1, 1, 1, "S"),
-    (1, 0, 0, "a2"), (1, 0, 1, "a2"), (1, 1, 0, "a2"), (1, 1, 1, "a2"), (1, 0, 0, "a4"), (1, 0, 0, "K1"),
-    (1, 0, 0, "K2"), (1, 0, 0, "r0"), (1, 0, 1, "a4"), (1, 0, 1, "K1"), (1, 0, 1, "K2"), (1, 0, 1, "r0"),
-    (1, 1, 0, "a4"), (1, 1, 0, "K1"), (1, 1, 0, "K2"), (1, 1, 0, "r0"), (1, 1, 1, "a4"), (1, 1, 1, "K1"),
-    (1, 1, 1, "K2"), (1, 1, 1, "r0"), (1, 0, 0, "r2"), (1, 0, 0, "W"), (1, 0, 2, "W"), (1, 0, 1, "r2"),
-    (1, 1, 0, "W"), (1, 1, 2, "W"), (1, 1, 0, "r2"), (1, 1, 1, "r2"), (2, 0, 0, "S"), (2, 0, 1, "S"),
-    (2, 1, 0, "S"), (2, 1, 1, "S"), (2, 0, 0, "a2"), (2, 0, 1, "a2"), (2, 1, 0, "a2"), (2, 1, 1, "a2"),
-    (2, 0, 0, "a4"), (2, 0, 0, "K1"), (2, 0, 0, "K2"), (2, 0, 0, "r0"), (2, 0, 1, "a4"), (2, 0, 1, "K1"),
+    (0, 0, 1, "S"), (0, 0, 0, "S"), (0, 1, 1, "S"), (0, 1, 0, "S"), (0, 0, 1, "a2"), (0, 0, 0, "a2"),
+    (0, 1, 1, "a2"), (0, 0, 1, "a3"), (0, 0, 0, "a3"), (0, 1, 0, "a2"), (0, 1, 1, "a3"), (0, 0, 0, "a4"),
+    (0, 0, 0, "K1"), (0, 0, 0, "K2"), (0, 1, 0, "a3"), (0, 0, 1, "a4"), (0, 0, 0, "r0"), (0, 0, 1, "K1"),
+    (0, 0, 1, "K2"), (0, 0, 1, "r0"), (0, 1, 0, "a4"), (0, 1, 0, "K1"), (0, 1, 0, "K2"), (0, 0, 0, "r1"),
+    (0, 1, 1, "a4"), (0, 1, 0, "r0"), (0, 0, 1, "r1"), (0, 1, 1, "K1"), (0, 1, 1, "K2"), (0, 1, 1, "r0"),
+    (0, 0, 0, "r2"), (0, 1, 0, "r1"), (0, 0, 1, "r2"), (0, 1, 1, "r1"), (0, 0, 0, "W"), (0, 1, 0, "r2"),
+    (0, 1, 1, "r2"), (1, 0, 0, "S"), (1, 0, 1, "S"), (1, 1, 0, "S"), (1, 0, 0, "a2"), (1, 1, 1, "S"),
+    (1, 0, 1, "a2"), (0, 1, 0, "W"), (1, 0, 0, "a3"), (1, 0, 1, "a3"), (1, 1, 0, "a2"), (1, 1, 1, "a2"),
+    (1, 0, 0, "a4"), (1, 0, 0, "K1"), (1, 0, 0, "K2"), (1, 1, 0, "a3"), (1, 0, 0, "r0"), (1, 0, 1, "a4"),
+    (1, 0, 1, "K1"), (1, 0, 1, "K2"), (1, 1, 1, "a3"), (1, 0, 1, "r0"), (1, 1, 0, "a4"), (1, 1, 0, "K1"),
+    (1, 1, 0, "K2"), (1, 0, 0, "r1"), (1, 1, 1, "a4"), (1, 1, 1, "K1"), (1, 1, 0, "r0"), (1, 0, 1, "r1"),
+    (1, 1, 1, "K2"), (1, 1, 1, "r0"), (1, 0, 0, "r2"), (1, 1, 0, "W"), (1, 1, 0, "r1"), (1, 0, 1, "r2"),
+    (1, 1, 1, "r1"), (0, 0, 2, "W"), (1, 1, 0, "r2"), (2, 0, 0, "S"), (1, 1, 1, "r2"), (2, 0, 1, "S"),
+    (2, 0, 0, "a2"), (2, 1, 0, "S"), (2, 1, 1, "S"), (2, 0, 1, "a2"), (1, 0, 2, "W"), (2, 0, 0, "a3"),
+    (2, 1, 0, "a2"), (2, 0, 1, "a3"), (2, 1, 1, "a2"), (2, 0, 0, "a4"), (2, 0, 0, "K1"), (2, 0, 0, "K2"),
+    (2, 1, 0, "a3"), (2, 0, 1, "a4"), (1, 0, 0, "W"), (2, 0, 0, "r0"), (2, 1, 1, "a3"), (2, 0, 1, "K1"),
     (2, 0, 1, "K2"), (2, 0, 1, "r0"), (2, 1, 0, "a4"), (2, 1, 0, "K1"), (2, 1, 0, "K2"), (2, 1, 0, "r0"),
-    (2, 1, 1, "a4"), (2, 1, 1, "K1"), (2, 1, 1, "K2"), (2, 1, 1, "r0"), (2, 0, 0, "r2"), (2, 0, 0, "W"),
-    (2, 0, 2, "W"), (2, 0, 1, "r2"), (2, 1, 0, "W"), (2, 1, 2, "W"), (2, 1, 0, "r2"), (2, 0, 1, "F"),
-    (2, 1, 1, "r2"), (2, 0, 0, "F"), (2, 1, 0, "F"), (2, 1, 1, "F"),
+    (2, 1, 1, "a4"), (2, 1, 1, "K1"), (2, 1, 1, "K2"), (2, 1, 1, "r0"), (0, 1, 2, "W"), (2, 0, 0, "r1"),
+    (2, 0, 0, "W"), (2, 0, 1, "r1"), (2, 1, 0, "r1"), (1, 1, 2, "W"), (2, 1, 1, "r1"), (2, 0, 2, "W"),
+    (2, 0, 0, "r2"), (2, 0, 1, "r2"), (2, 1, 0, "r2"), (2, 1, 1, "r2"), (2, 1, 0, "W"), (2, 1, 2, "W"),
+    (2, 1, 0, "F"), (2, 0, 1, "F"), (2, 0, 0, "F"), (2, 1, 1, "F"),
 )
 
 
@@ -66,7 +70,7 @@
     out_s, out_c, out_gin, out_gout,
     st, ct, fs, fc, w_in, w_out, gain, gain_above,
     held, got, ga, gb, hid, bpre, pa, pb,
-    big_r, slope, summed, summed_b, small_r,
+    big_p, slope, summed, summed_b, small_r,
     ssem, rsem, lsem,
 ):
     ticks = feed_s.shape[0] + 1
@@ -363,7 +367,8 @@
             acc[0, cols, :] = part if t == 0 else acc[0, cols, :] + part
             return carry
 
-        lax.fori_loop(lo, lo + count, body, 0)
+        first = lo * 256 // GRAD_TILE
+        lax.fori_loop(first, first + count * 256 // GRAD_TILE, body, 0)
 
     chunks = {}
     for t in range(ticks):
@@ -416,7 +421,7 @@
     hbm = pl.BlockSpec(memory_space=pltpu.HBM)
     vmem = pl.BlockSpec(memory_space=pltpu.VMEM)
     outs = (streams.shape, cotangents.shape, w_in.shape, w_out.shape)
-    return pl.pallas_call(
+    held_outs = pl.pallas_call(
         kernel,
         out_shape=tuple(pltpu.VMEM(s, F32) for s in outs),
         in_specs=[hbm] * 7,
@@ -438,7 +443,7 @@
             pltpu.VMEM((q, n, hidden), BF),
             pltpu.VMEM(blocks, BF),
             pltpu.VMEM(blocks, BF),
-            pltpu.VMEM((q, 2, 3, SIDE, r, width), BF),
+            pltpu.VMEM((q, 2, 8, 2, r, width), BF),
             pltpu.VMEM((CHUNKS, n, hidden), F32),
             pltpu.VMEM((CHUNKS, 2, SIDE, r, width), F32),
             pltpu.VMEM((q, 2, SIDE, r, width), BF),
@@ -451,6 +456,29 @@
             collective_id=0, has_side_effects=True, vmem_limit_bytes=50 * 1024 * 1024
         ),
     )(streams, cotangents, feed_streams, feed_cotangents, w_in, w_out, gain)
+    parts = [(2, k) for k in range(4)] + [(3, k) for k in range(4)] + [(0, 0), (1, 0)]
+
+    def store(*refs):
+        outs_in, outs_to, sems = refs[:4], refs[4:8], refs[8]
+        copies = []
+        for i, (which, k) in enumerate(parts):
+            src, dst = outs_in[which].at[0], outs_to[which].at[0]
+            if which >= 2:
+                span = pl.ds(k * (src.shape[0] // 4), src.shape[0] // 4)
+                src, dst = src.at[span], dst.at[span]
+            copies.append(pltpu.make_async_copy(src, dst, sems.at[i]))
+            copies[-1].start()
+        for copy in copies:
+            copy.wait()
+
+    return pl.pallas_call(
+        store,
+        out_shape=tuple(jax.ShapeDtypeStruct(s, F32) for s in outs),
+        in_specs=[vmem] * 4,
+        out_specs=(hbm,) * 4,
+        scratch_shapes=[pltpu.SemaphoreType.DMA((len(parts),))],
+        compiler_params=pltpu.CompilerParams(vmem_limit_bytes=4 * 1024 * 1024),
+    )(*[pltpu.with_memory_space_constraint(a, pltpu.VMEM) for a in held_outs])
 
 
 def solution(mesh):

time: 118 us -> 110 us (0.932)
  local copies, waits for them, and re-layouts: 5.43 us -> 0 us
  Pallas kernels: 111 us -> 108 us
    pallas_call x1, Pallas kernels: 111 us -> 104 us  [shards(): pl.pallas_call(kernel, out_shape=tuple((pltpu.VMEM(s, F32) for s in outs)...]
    unnamed x4 -> x0, local copies, waits for them, and re-layouts: 5.43 us -> none
    pallas_call x0 -> x1, Pallas kernels: none -> 3.51 us  [shards(): pl.pallas_call(store, out_shape=tuple((jax.ShapeDtypeStruct(s, F32) for s...]
where the time goes in v3:
time: 110 us; the launch traced here: 109 us
  Pallas kernels  108 us (98%)
    pallas_call x1, Pallas kernels, shards(): pl.pallas_call(kernel, out_shape=tuple((pltpu.VMEM(s, F32) for s in outs)...  104 us
    pallas_call x1, Pallas kernels, shards(): pl.pallas_call(store, out_shape=tuple((jax.ShapeDtypeStruct(s, F32) for s...  3.51 us

profile of v3, /device:TPU:8, one launch (start us, length us, event | category | flops | bytes accessed | tf_op | source)
XLA Modules:
  0.0 108.7 jit_solution(11909984422561425560)
XLA Ops:
  0.6 104.4 %shard_map.102 = (f32[1,2,32,1024]{3,2,1,0:T(8,128)S(1)}, f32[1,2,32,1024]{3,2,1,0:T(8,128)S(1)}, f32[1,1024,1024]{2,1,0:T(8,128)S(1)}, f32[1,1024,1024]{2,1,0:T(8,128)S(1)}) custom-call(f32[1,2,32,1024]{3,2,1,0:T(8,128)} %streams.1, f32[1,2,32,1024]{3,2,1,0:T(8,128)} %cots.1, f32[2,2,32,1024]{3,2,1,0:T(8,128)} %feed_s.1, f32[2,2,32,1024]{3,2,1,0:T(8,128)} %feed_c.1, ...), custom_call_target="tpu_custom_call" | custom-call | tf_op jit(solution)/shard_map/pallas_call | solution.py:424
  105.0 3.5 %shard_map.103 = (f32[1,2,32,1024]{3,2,1,0:T(8,128)}, f32[1,2,32,1024]{3,2,1,0:T(8,128)}, f32[1,1024,1024]{2,1,0:T(8,128)}, f32[1,1024,1024]{2,1,0:T(8,128)}) custom-call(f32[1,2,32,1024]{3,2,1,0:T(8,128)S(1)} %get-tuple-element.8.refs_0_, f32[1,2,32,1024]{3,2,1,0:T(8,128)S(1)} %get-tuple-element.9.refs_1_, f32[1,1024,1024]{2,1,0:T(8,128)S(1)} %get-tuple-element.10.refs_2_, ...), custom_call_target="tpu_custom_call" | custom-call | tf_op jit(solution)/shard_map/pallas_call | solution.py:474

commit v4 on v3

--- a/solution.py
+++ b/solution.py
@@ -37,27 +37,27 @@
 
 
 ORDER = (
-    (0, 0, 1, "S"), (0, 0, 0, "S"), (0, 1, 1, "S"), (0, 1, 0, "S"), (0, 0, 1, "a2"), (0, 0, 0, "a2"),
-    (0, 1, 1, "a2"), (0, 0, 1, "a3"), (0, 0, 0, "a3"), (0, 1, 0, "a2"), (0, 1, 1, "a3"), (0, 0, 0, "a4"),
-    (0, 0, 0, "K1"), (0, 0, 0, "K2"), (0, 1, 0, "a3"), (0, 0, 1, "a4"), (0, 0, 0, "r0"), (0, 0, 1, "K1"),
+    (0, 0, 0, "S"), (0, 1, 0, "S"), (0, 0, 1, "S"), (0, 1, 1, "S"), (0, 0, 0, "a2"), (0, 0, 1, "a2"),
+    (0, 0, 0, "a3"), (0, 1, 0, "a2"), (0, 0, 1, "a3"), (0, 1, 1, "a2"), (0, 0, 0, "a4"), (0, 0, 0, "K1"),
+    (0, 0, 0, "K2"), (0, 1, 0, "a3"), (0, 0, 0, "r0"), (0, 1, 1, "a3"), (0, 0, 1, "a4"), (0, 0, 1, "K1"),
     (0, 0, 1, "K2"), (0, 0, 1, "r0"), (0, 1, 0, "a4"), (0, 1, 0, "K1"), (0, 1, 0, "K2"), (0, 0, 0, "r1"),
-    (0, 1, 1, "a4"), (0, 1, 0, "r0"), (0, 0, 1, "r1"), (0, 1, 1, "K1"), (0, 1, 1, "K2"), (0, 1, 1, "r0"),
-    (0, 0, 0, "r2"), (0, 1, 0, "r1"), (0, 0, 1, "r2"), (0, 1, 1, "r1"), (0, 0, 0, "W"), (0, 1, 0, "r2"),
-    (0, 1, 1, "r2"), (1, 0, 0, "S"), (1, 0, 1, "S"), (1, 1, 0, "S"), (1, 0, 0, "a2"), (1, 1, 1, "S"),
-    (1, 0, 1, "a2"), (0, 1, 0, "W"), (1, 0, 0, "a3"), (1, 0, 1, "a3"), (1, 1, 0, "a2"), (1, 1, 1, "a2"),
-    (1, 0, 0, "a4"), (1, 0, 0, "K1"), (1, 0, 0, "K2"), (1, 1, 0, "a3"), (1, 0, 0, "r0"), (1, 0, 1, "a4"),
-    (1, 0, 1, "K1"), (1, 0, 1, "K2"), (1, 1, 1, "a3"), (1, 0, 1, "r0"), (1, 1, 0, "a4"), (1, 1, 0, "K1"),
-    (1, 1, 0, "K2"), (1, 0, 0, "r1"), (1, 1, 1, "a4"), (1, 1, 1, "K1"), (1, 1, 0, "r0"), (1, 0, 1, "r1"),
-    (1, 1, 1, "K2"), (1, 1, 1, "r0"), (1, 0, 0, "r2"), (1, 1, 0, "W"), (1, 1, 0, "r1"), (1, 0, 1, "r2"),
-    (1, 1, 1, "r1"), (0, 0, 2, "W"), (1, 1, 0, "r2"), (2, 0, 0, "S"), (1, 1, 1, "r2"), (2, 0, 1, "S"),
-    (2, 0, 0, "a2"), (2, 1, 0, "S"), (2, 1, 1, "S"), (2, 0, 1, "a2"), (1, 0, 2, "W"), (2, 0, 0, "a3"),
-    (2, 1, 0, "a2"), (2, 0, 1, "a3"), (2, 1, 1, "a2"), (2, 0, 0, "a4"), (2, 0, 0, "K1"), (2, 0, 0, "K2"),
-    (2, 1, 0, "a3"), (2, 0, 1, "a4"), (1, 0, 0, "W"), (2, 0, 0, "r0"), (2, 1, 1, "a3"), (2, 0, 1, "K1"),
+    (0, 1, 1, "a4"), (0, 1, 0, "r0"), (0, 1, 1, "K1"), (0, 0, 1, "r1"), (0, 1, 1, "K2"), (0, 1, 1, "r0"),
+    (0, 0, 0, "r2"), (0, 1, 0, "r1"), (0, 0, 2, "W"), (0, 1, 1, "r1"), (0, 0, 1, "r2"), (0, 1, 0, "r2"),
+    (0, 1, 0, "W"), (1, 0, 0, "S"), (0, 1, 1, "r2"), (1, 0, 1, "S"), (0, 1, 2, "W"), (1, 0, 0, "a2"),
+    (1, 1, 0, "S"), (1, 0, 1, "a2"), (1, 1, 1, "S"), (1, 0, 0, "a3"), (1, 1, 0, "a2"), (1, 0, 1, "a3"),
+    (1, 1, 1, "a2"), (1, 0, 0, "a4"), (1, 0, 0, "K1"), (1, 0, 0, "K2"), (1, 1, 0, "a3"), (1, 0, 0, "r0"),
+    (1, 0, 1, "a4"), (1, 0, 1, "K1"), (1, 1, 1, "a3"), (1, 0, 1, "K2"), (1, 0, 1, "r0"), (1, 1, 0, "a4"),
+    (1, 1, 0, "K1"), (1, 1, 0, "K2"), (1, 0, 0, "r1"), (1, 1, 1, "a4"), (1, 1, 0, "r0"), (1, 1, 1, "K1"),
+    (1, 0, 1, "r1"), (1, 1, 1, "K2"), (1, 1, 1, "r0"), (1, 0, 0, "r2"), (1, 1, 0, "r1"), (1, 0, 1, "r2"),
+    (1, 1, 1, "r1"), (1, 1, 0, "r2"), (2, 0, 0, "S"), (1, 1, 1, "r2"), (2, 0, 1, "S"), (2, 1, 0, "S"),
+    (2, 0, 0, "a2"), (1, 0, 2, "W"), (2, 1, 1, "S"), (2, 0, 1, "a2"), (2, 0, 0, "a3"), (1, 1, 2, "W"),
+    (2, 1, 0, "a2"), (2, 0, 1, "a3"), (1, 1, 0, "W"), (2, 1, 1, "a2"), (2, 0, 0, "a4"), (2, 0, 0, "K1"),
+    (2, 0, 0, "K2"), (2, 1, 0, "a3"), (2, 0, 1, "a4"), (2, 0, 1, "K1"), (2, 1, 1, "a3"), (2, 0, 0, "r0"),
     (2, 0, 1, "K2"), (2, 0, 1, "r0"), (2, 1, 0, "a4"), (2, 1, 0, "K1"), (2, 1, 0, "K2"), (2, 1, 0, "r0"),
-    (2, 1, 1, "a4"), (2, 1, 1, "K1"), (2, 1, 1, "K2"), (2, 1, 1, "r0"), (0, 1, 2, "W"), (2, 0, 0, "r1"),
-    (2, 0, 0, "W"), (2, 0, 1, "r1"), (2, 1, 0, "r1"), (1, 1, 2, "W"), (2, 1, 1, "r1"), (2, 0, 2, "W"),
-    (2, 0, 0, "r2"), (2, 0, 1, "r2"), (2, 1, 0, "r2"), (2, 1, 1, "r2"), (2, 1, 0, "W"), (2, 1, 2, "W"),
-    (2, 1, 0, "F"), (2, 0, 1, "F"), (2, 0, 0, "F"), (2, 1, 1, "F"),
+    (2, 1, 1, "a4"), (2, 1, 1, "K1"), (2, 1, 1, "K2"), (2, 1, 1, "r0"), (0, 0, 0, "W"), (2, 0, 1, "r1"),
+    (2, 0, 0, "r1"), (2, 0, 2, "W"), (2, 1, 0, "r1"), (2, 1, 0, "W"), (2, 1, 1, "r1"), (2, 0, 0, "r2"),
+    (2, 1, 2, "W"), (2, 0, 1, "r2"), (2, 1, 0, "r2"), (2, 1, 1, "r2"), (1, 0, 0, "W"), (2, 0, 0, "W"),
+    (2, 0, 0, "F"), (2, 1, 0, "F"), (2, 0, 1, "F"), (2, 1, 1, "F"),
 )
 
 
@@ -100,15 +100,12 @@
         return copy
 
     first_loads = [load(0, streams.at[0], st), load(1, cots.at[0], ct), load(2, gain_hbm, gain)]
-    weight_loads = [load(3, w_in_hbm.at[0], w_in), load(4, w_out_hbm.at[0], w_out)]
-    feed_loads = [load(5, feed_s, fs), load(6, feed_c, fc)]
 
     barrier = pltpu.get_barrier_semaphore()
     peers = [axis(by, s) for s in (sec, above, below) for axis in (along_x, along_z) for by in STEPS]
     peers += [along_x(0, above), along_x(0, below)]
     for peer in peers:
         pl.semaphore_signal(barrier, inc=1, device_id=peer, device_id_type=MESH)
-    pl.semaphore_wait(barrier, len(peers))
     for copy in first_loads:
         copy.wait()
 
@@ -277,7 +274,7 @@
             self.rows = pl.ds(c * r, r)
             self.lanes = (Lane(t, self.q, 0), Lane(t, self.q, 1))
 
-        def start(self, which):
+        def prepare(self, which):
             t, q = self.t, self.q
             mine = held.at[q]
             two = pl.ds(2 * which, 2)
@@ -299,9 +296,15 @@
                 ga[q, z, x] = (normalized(mine[0])[0] * gain[...]).astype(BF)
             else:
                 gb[q, z, x] = mine[3].astype(BF)
+
+        def start(self, which):
+            t, q = self.t, self.q
+            two = pl.ds(2 * which, 2)
+            if t > 0:
+                self.prepare(which)
             self.lanes[which].a0()
             if t < ticks - 1:
-                send(q, PASS + which, mine.at[two], got.at[q, two], along_x(0, below))
+                send(q, PASS + which, held.at[q, two], got.at[q, two], along_x(0, below))
 
         def finish(self, which):
             mine = held.at[self.q]
@@ -385,14 +388,26 @@
         for copy in copies:
             copy.wait()
 
+    for c in range(CHUNKS):
+        for which in (0, 1):
+            chunks[0, c].prepare(which)
+    pl.semaphore_wait(barrier, len(peers))
+    later = []
+
+    def load_rest():
+        later.extend([load(3, w_in_hbm.at[0], w_in), load(4, w_out_hbm.at[0], w_out)])
+        later.extend([load(5, feed_s, fs), load(6, feed_c, fc)])
+
     for t, c, which, what in order(ticks):
+        if what != "S":
+            once("rest", load_rest)
         if what == "W":
             weight_piece(t, c, which, 2)
             continue
         chunk = chunks[t, c]
         if what == "S":
             if t > 0:
-                once("feed", lambda: wait_all(feed_loads))
+                once("feed", lambda: wait_all(later[2:]))
                 if which == 1:
                     once("gain", lambda: arrived(0, PASS + 2, gain_above))
             chunk.start(which)
@@ -400,7 +415,7 @@
         elif what == "F":
             chunk.finish(which)
         elif what == "K1":
-            once("weights", lambda: wait_all(weight_loads))
+            once("weights", lambda: wait_all(later[:2]))
             chunk.k1(which)
         elif what == "K2":
             chunk.k2(which)

time: 110 us -> 110 us (level)
  no operation moved by 1% of the time
where the time goes in v4:
time: 110 us; the launch traced here: 109 us
  Pallas kernels  109 us (99%)
    pallas_call x1, Pallas kernels, shards(): pl.pallas_call(kernel, out_shape=tuple((pltpu.VMEM(s, F32) for s in outs)...  105 us
    pallas_call x1, Pallas kernels, shards(): pl.pallas_call(store, out_shape=tuple((jax.ShapeDtypeStruct(s, F32) for s...  3.51 us

profile of v4, /device:TPU:8, one launch (start us, length us, event | category | flops | bytes accessed | tf_op | source)
XLA Modules:
  0.0 109.3 jit_solution(2323816288028171384)
XLA Ops:
  0.6 105.0 %shard_map.102 = (f32[1,2,32,1024]{3,2,1,0:T(8,128)S(1)}, f32[1,2,32,1024]{3,2,1,0:T(8,128)S(1)}, f32[1,1024,1024]{2,1,0:T(8,128)S(1)}, f32[1,1024,1024]{2,1,0:T(8,128)S(1)}) custom-call(f32[1,2,32,1024]{3,2,1,0:T(8,128)} %streams.1, f32[1,2,32,1024]{3,2,1,0:T(8,128)} %cots.1, f32[2,2,32,1024]{3,2,1,0:T(8,128)} %feed_s.1, f32[2,2,32,1024]{3,2,1,0:T(8,128)} %feed_c.1, ...), custom_call_target="tpu_custom_call" | custom-call | tf_op jit(solution)/shard_map/pallas_call | solution.py:439
  105.6 3.5 %shard_map.103 = (f32[1,2,32,1024]{3,2,1,0:T(8,128)}, f32[1,2,32,1024]{3,2,1,0:T(8,128)}, f32[1,1024,1024]{2,1,0:T(8,128)}, f32[1,1024,1024]{2,1,0:T(8,128)}) custom-call(f32[1,2,32,1024]{3,2,1,0:T(8,128)S(1)} %get-tuple-element.8.refs_0_, f32[1,2,32,1024]{3,2,1,0:T(8,128)S(1)} %get-tuple-element.9.refs_1_, f32[1,1024,1024]{2,1,0:T(8,128)S(1)} %get-tuple-element.10.refs_2_, ...), custom_call_target="tpu_custom_call" | custom-call | tf_op jit(solution)/shard_map/pallas_call | solution.py:489

commit v5 on v4

--- a/solution.py
+++ b/solution.py
@@ -471,7 +471,7 @@
             collective_id=0, has_side_effects=True, vmem_limit_bytes=50 * 1024 * 1024
         ),
     )(streams, cotangents, feed_streams, feed_cotangents, w_in, w_out, gain)
-    parts = [(2, k) for k in range(4)] + [(3, k) for k in range(4)] + [(0, 0), (1, 0)]
+    parts = [(2, k) for k in range(8)] + [(3, k) for k in range(8)] + [(0, 0), (1, 0)]
 
     def store(*refs):
         outs_in, outs_to, sems = refs[:4], refs[4:8], refs[8]
@@ -479,7 +479,7 @@
         for i, (which, k) in enumerate(parts):
             src, dst = outs_in[which].at[0], outs_to[which].at[0]
             if which >= 2:
-                span = pl.ds(k * (src.shape[0] // 4), src.shape[0] // 4)
+                span = pl.ds(k * (src.shape[0] // 8), src.shape[0] // 8)
                 src, dst = src.at[span], dst.at[span]
             copies.append(pltpu.make_async_copy(src, dst, sems.at[i]))
             copies[-1].start()

time: 110 us -> 110 us (level)
  no operation moved by 1% of the time
where the time goes in v5:
time: 110 us; the launch traced here: 109 us
  Pallas kernels  109 us (99%)
    pallas_call x1, Pallas kernels, shards(): pl.pallas_call(kernel, out_shape=tuple((pltpu.VMEM(s, F32) for s in outs)...  105 us
    pallas_call x1, Pallas kernels, shards(): pl.pallas_call(store, out_shape=tuple((jax.ShapeDtypeStruct(s, F32) for s...  3.58 us

profile of v5, /device:TPU:8, one launch (start us, length us, event | category | flops | bytes accessed | tf_op | source)
XLA Modules:
  0.0 109.4 jit_solution(11242736032352903994)
XLA Ops:
  0.6 105.0 %shard_map.102 = (f32[1,2,32,1024]{3,2,1,0:T(8,128)S(1)}, f32[1,2,32,1024]{3,2,1,0:T(8,128)S(1)}, f32[1,1024,1024]{2,1,0:T(8,128)S(1)}, f32[1,1024,1024]{2,1,0:T(8,128)S(1)}) custom-call(f32[1,2,32,1024]{3,2,1,0:T(8,128)} %streams.1, f32[1,2,32,1024]{3,2,1,0:T(8,128)} %cots.1, f32[2,2,32,1024]{3,2,1,0:T(8,128)} %feed_s.1, f32[2,2,32,1024]{3,2,1,0:T(8,128)} %feed_c.1, ...), custom_call_target="tpu_custom_call" | custom-call | tf_op jit(solution)/shard_map/pallas_call | solution.py:439
  105.6 3.6 %shard_map.103 = (f32[1,2,32,1024]{3,2,1,0:T(8,128)}, f32[1,2,32,1024]{3,2,1,0:T(8,128)}, f32[1,1024,1024]{2,1,0:T(8,128)}, f32[1,1024,1024]{2,1,0:T(8,128)}) custom-call(f32[1,2,32,1024]{3,2,1,0:T(8,128)S(1)} %get-tuple-element.8.refs_0_, f32[1,2,32,1024]{3,2,1,0:T(8,128)S(1)} %get-tuple-element.9.refs_1_, f32[1,1024,1024]{2,1,0:T(8,128)S(1)} %get-tuple-element.10.refs_2_, ...), custom_call_target="tpu_custom_call" | custom-call | tf_op jit(solution)/shard_map/pallas_call | solution.py:489
